TPU v7x, 32 devices: a whole 2x2x4 slice. The times are simulated.
32 devices in a mesh: row: 4 (over y, x), col: 8 (over z, core).
Axes of the slice: x: 2, y: 2, z: 4, core: 2. Of those that a mesh axis runs over, the one named last changes fastest.
Arguments:
- new_row: float32 [128, 96, 128], P('row', 'col'), may hold values from -4 to 4
- history: float32 [96, 96, 128, 128], P('row', 'col'), may hold values from -0.0546875 to 0.0546875
- hamiltonian: float32 [128, 128], replicated, may hold values from -0.5 to 0.5
Outputs:
- rows_out: float32 [3, 128, 96, 128], P(None, 'row', 'col')
All inputs are finite; a program needn't handle non-finite values.
Results may differ from a plain program's by a relative error of at most 0.00026.
Values sent between devices are 32-bit elements; how exact they have to be, the bound alone decides.
No kernel may reach another device: no remote copies, remote signals or barrier semaphores. Data moves between devices by JAX's collectives and lax.ppermute only.
A program may use at most 128 MiB of HBM per device.

v0:
```python
import functools

import jax
import jax.numpy as jnp
from jax import lax
from jax.experimental import pallas as pl
from jax.experimental.pallas import tpu as pltpu
from jax.sharding import PartitionSpec as P


STEPS = 3
CORES = 2
CHUNKS = 2

time_step = 0.2

AXES = ("row", "col")
VMEM = pltpu.VMEM


def split_kernel(slots, h_hbm, hi_ref, lo_ref, buf, sem):
    times, cols, depth, width = h_hbm.shape
    piece = cols // CHUNKS

    def copy(s):
        return pltpu.make_async_copy(h_hbm.at[s], buf.at[s % slots], sem.at[s % slots])

    for s in range(slots - 1):
        copy(s).start()

    def body(s, carry):
        @pl.when(s + slots - 1 < times)
        def _():
            copy(s + slots - 1).start()

        copy(s).wait()
        half, t = s // cols, s % cols
        order = ((t // piece) * CORES + half) * piece + t % piece
        rows = pl.ds(pl.multiple_of(order * depth, depth), depth)
        for t in range(cols):
            tile = buf[s % slots, t]
            high = tile.astype(jnp.bfloat16)
            at = slice(t * width, (t + 1) * width)
            hi_ref[rows, at] = high
            lo_ref[rows, at] = (tile - high.astype(jnp.float32)).astype(jnp.bfloat16)
        return carry

    lax.fori_loop(0, times, body, 0)


def split_history(history):
    times, cols, depth, width = history.shape
    slots = 6
    shape = (times * depth, cols * width)
    history = pltpu.with_memory_space_constraint(history, pltpu.HBM)
    return pl.pallas_call(
        functools.partial(split_kernel, slots),
        in_specs=[pl.BlockSpec(memory_space=pltpu.HBM)],
        out_specs=[pl.BlockSpec(memory_space=VMEM)] * 2,
        out_shape=[pltpu.VMEM(shape, jnp.bfloat16)] * 2,
        scratch_shapes=[
            pltpu.VMEM((slots, cols, depth, width), jnp.float32),
            pltpu.SemaphoreType.DMA((slots,)),
        ],
        compiler_params=pltpu.CompilerParams(vmem_limit_bytes=6 << 20),
        cost_estimate=pl.CostEstimate(
            flops=0, bytes_accessed=history.size * 8, transcendentals=0
        ),
        name="split_history",
    )(history)


def position():
    r = lax.axis_index("row")
    c = lax.axis_index("col")
    return r, c // CORES, c % CORES


def origins(turns, k):
    own = [jnp.where(k == 0, turn[0], turn[1]) for turn in turns]
    theirs = [jnp.where(k == 0, turn[1], turn[0]) for turn in turns]
    return [(d, k) for d in own] + [(d, 1 - k) for d in theirs]


def fill(turns, blocks, sig):
    _, _, k = position()
    halves, cols, rows, depth = blocks[0].shape
    total = len(blocks) * rows
    for b, (_, first) in enumerate(origins(turns, k)):
        for half in range(halves):
            for t in range(cols):
                x = blocks[b][first ^ half, t]
                x = x * x * x
                high = x.astype(jnp.bfloat16)
                s = half * cols + t
                at = slice(s * depth, (s + 1) * depth)
                sig[b * rows : (b + 1) * rows, at] = high
                sig[total + b * rows : total + (b + 1) * rows, at] = (
                    x - high.astype(jnp.float32)
                ).astype(jnp.bfloat16)


def product(sig, hi, lo, inner, at):
    total = sig.shape[0] // 2
    both = jnp.dot(sig[...], hi[inner, at], preferred_element_type=jnp.float32)
    rest = jnp.dot(
        sig[0:total, :], lo[inner, at], preferred_element_type=jnp.float32
    )
    return both[0:total] + both[total:] + rest


def spread(turns, value, out, t0, group):
    r, m, k = position()
    rows, width = out.shape[2:]
    for b, (d, _) in enumerate(origins(turns, k)):
        for t in range(group):
            out[m ^ d ^ r, t0 + t] = value[
                b * rows : (b + 1) * rows, t * width : (t + 1) * width
            ]


def first_kernel(turns, panels, *refs):
    blocks = refs[:panels]
    hi, lo, acc, _, _, sig = refs[panels:]
    fill(turns, blocks, sig)
    inner = slice(0, sig.shape[1])
    step = 256
    for n in range(0, acc.shape[1], step):
        at = slice(n, n + step)
        acc[:, at] = product(sig, hi, lo, inner, at)


def second_kernel(turns, panels, *refs):
    blocks = refs[:panels]
    acc, hi, lo, out, sig, _, _ = refs[panels:]
    fill(turns, blocks, sig)
    finish(turns, 0, sig, acc, hi, lo, out)


def third_kernel(turns, sig, acc, hi, lo, out, hi_out, lo_out):
    finish(turns, 1, sig, acc, hi, lo, out)


def finish(turns, chunk, sig, acc, hi, lo, out):
    depth = sig.shape[1]
    inner = slice(depth, 2 * depth)
    cols, _, width = out.shape[1:]
    group = 2
    for t0 in range(0, cols, group):
        n = (chunk * cols + t0) * width
        at = slice(n, n + group * width)
        value = acc[:, at] + product(sig, hi, lo, inner, at)
        spread(turns, value, out, t0, group)


def call(kernel, inputs, hi, lo, outs, scratch, flops):
    count = len(inputs)
    return pl.pallas_call(
        kernel,
        in_specs=[pl.BlockSpec(memory_space=VMEM)] * (count + 2),
        out_specs=[pl.BlockSpec(memory_space=VMEM)] * (len(outs) + 2),
        out_shape=outs
        + [pltpu.VMEM(hi.shape, hi.dtype), pltpu.VMEM(lo.shape, lo.dtype)],
        input_output_aliases={count: len(outs), count + 1: len(outs) + 1},
        scratch_shapes=scratch,
        compiler_params=pltpu.CompilerParams(vmem_limit_bytes=6 << 20),
        cost_estimate=pl.CostEstimate(
            flops=flops, bytes_accessed=4 << 20, transcendentals=0
        ),
    )(*inputs, hi, lo)


def small_call(kernel, like, inputs):
    return pl.pallas_call(
        kernel,
        in_specs=[pl.BlockSpec(memory_space=VMEM)] * len(inputs),
        out_specs=pl.BlockSpec(memory_space=VMEM),
        out_shape=jax.ShapeDtypeStruct(like.shape, like.dtype),
        compiler_params=pltpu.CompilerParams(vmem_limit_bytes=4 << 20),
        cost_estimate=pl.CostEstimate(
            flops=0, bytes_accessed=1 << 20, transcendentals=0
        ),
    )(*inputs)


def base_kernel(value, hamiltonian, out):
    x = value[...]
    kinetic = jnp.dot(
        x.reshape(-1, x.shape[-1]),
        hamiltonian[...],
        precision=lax.Precision.HIGHEST,
        preferred_element_type=jnp.float32,
    )
    out[...] = x - time_step * kinetic.reshape(x.shape)


def own_kernel(base, part, out):
    out[...] = base[...] - time_step * part[...]


def pairs(nrow, ncol, target):
    listed = []
    for r in range(nrow):
        for c in range(ncol):
            to_r, to_c = target(r, c // CORES, c % CORES)
            listed.append((r * ncol + c, to_r * ncol + to_c))
    return listed


def per_device(nrow, ncol, new_row, history, hamiltonian):
    def move(value, target):
        return lax.ppermute(value, AXES, pairs(nrow, ncol, target))

    def partner(value):
        return move(value, lambda r, m, k: (r, m * CORES + 1 - k))

    turns = []
    for d in range(nrow // 4):
        turns += [(d, d ^ nrow // 2), (d ^ nrow - 1, d ^ nrow // 2 ^ nrow - 1)]
    sends = [
        lambda r, m, k, turn=turn: (m, (r ^ turn[k]) * CORES + k) for turn in turns
    ]

    def gather(value, other):
        both = jnp.stack([value, other])
        mine = [move(both, send) for send in sends]
        return mine + [partner(block) for block in mine]

    def reduce(parts):
        return [parts[0]] + [
            move(parts[x], lambda r, m, k, x=x: (r ^ x, m * CORES + k))
            for x in range(1, nrow)
        ]

    hi, lo = split_history(history)
    start = jnp.transpose(new_row, (1, 0, 2))
    cols, rows, width = start.shape
    piece = cols // CHUNKS
    swapped = partner(start)
    state = [start[a * piece : (a + 1) * piece] for a in range(CHUNKS)]
    other = [swapped[a * piece : (a + 1) * piece] for a in range(CHUNKS)]
    total = nrow * rows
    depth = hi.shape[0] // CHUNKS
    part = jax.ShapeDtypeStruct((nrow, piece, rows, width), jnp.float32)
    acc_type = jax.ShapeDtypeStruct((total, hi.shape[1]), jnp.float32)
    sig_type = jax.ShapeDtypeStruct((2 * total, depth), jnp.bfloat16)
    flops = 3 * total * depth * hi.shape[1]
    rows_out = jnp.zeros((STEPS, cols, rows, width), jnp.float32)
    for n in range(STEPS):
        if n > 0:
            other = [partner(state[a]) for a in range(CHUNKS)]
        blocks = [gather(state[a], other[a]) for a in range(CHUNKS)]
        base = []
        for value in state:
            base.append(small_call(base_kernel, value, [value, hamiltonian]))
        acc, hi, lo = call(
            functools.partial(first_kernel, turns, nrow),
            blocks[0], hi, lo, [acc_type],
            [pltpu.VMEM(sig_type.shape, sig_type.dtype)], 2 * flops,
        )
        parts0, sig, hi, lo = call(
            functools.partial(second_kernel, turns, nrow),
            blocks[1] + [acc], hi, lo, [part, sig_type], [], flops,
        )
        parts1, hi, lo = call(
            functools.partial(third_kernel, turns),
            [sig, acc], hi, lo, [part], [], flops,
        )
        base[0] = small_call(own_kernel, state[0], [base[0], parts0[0]])
        for a, parts in enumerate((parts0, parts1)):
            arrived = reduce(parts)
            total = sum(arrived[2:], arrived[1])
            if a:
                total = total + arrived[0]
            state[a] = base[a] - time_step * total
            rows_out = lax.dynamic_update_slice(
                rows_out, state[a][None], (n, a * piece, 0, 0)
            )
    return jnp.transpose(rows_out, (0, 2, 1, 3))


def solution(mesh):
    placed = (P("row", "col", None), P("row", "col", None, None), P())
    return jax.shard_map(
        functools.partial(per_device, mesh.shape["row"], mesh.shape["col"]),
        mesh=mesh,
        in_specs=placed,
        out_specs=P(None, "row", "col", None),
        check_vma=False,
    )
```

profile of v0, /device:TPU:0, one launch (start us, length us, event | category | flops | bytes accessed | tf_op | source)
XLA Modules:
  0.0 129.0 jit_solution(11965143742550752195)
XLA Ops:
  0.5 1.0 fusion.8
  1.8 5.0 %collective-permute-start.6 = (f32[2,6,32,128]{3,2,1,0:T(8,128)S(1)}, f32[2,6,32,128]{3,2,1,0:T(8,128)S(1)}, u32[]{:S(2)}, u32[]{:S(2)}) collective-permute-start(f32[2,6,32,128]{3,2,1,0:T(8,128)S(1)} %pad_maximum_fusion.1), channel_id=1, source_target_pairs={{0,6},{1,3},{2,14},{3,11},{4,22},{5,19},{6,30},{7,27},{8,4},{9,1},... | collective-permute-start | bytes 589832 | tf_op jit(solution)/shard_map/ppermute | solution.py:212
  7.5 3.7 %collective-permute-start.2 = (f32[2,6,32,128]{3,2,1,0:T(8,128)S(1)}, f32[2,6,32,128]{3,2,1,0:T(8,128)S(1)}, u32[]{:S(2)}, u32[]{:S(2)}) collective-permute-start(f32[2,6,32,128]{3,2,1,0:T(8,128)S(1)} %pad_maximum_fusion), channel_id=1, source_target_pairs={{0,6},{1,3},{2,14},{3,11},{4,22},{5,19},{6,30},{7,27},{8,4},{9,1},... | collective-permute-start | bytes 589832 | tf_op jit(solution)/shard_map/ppermute | solution.py:212
  11.9 2.0 %collective-permute-start.8 = (f32[2,6,32,128]{3,2,1,0:T(8,128)S(1)}, f32[2,6,32,128]{3,2,1,0:T(8,128)S(1)}, u32[]{:S(2)}, u32[]{:S(2)}) collective-permute-start(f32[2,6,32,128]{3,2,1,0:T(8,128)S(1)} %collective-permute-done.6.refs_1_), channel_id=1, source_target_pairs={{0,1},{1,0},{2,3},{3,2},{4,5},{5,4},{6,7},{7,6},{8,9},{9,8},{10,11... | collective-permute-start | bytes 589832 | tf_op jit(solution)/shard_map/ppermute | solution.py:212
  14.0 3.9 %collective-permute-done.2.refs_1_ = f32[2,6,32,128]{3,2,1,0:T(8,128)S(1)} collective-permute-done((f32[2,6,32,128]{3,2,1,0:T(8,128)S(1)}, f32[2,6,32,128]{3,2,1,0:T(8,128)S(1)}, u32[]{:S(2)}, u32[]{:S(2)}) %collective-permute-start.2) | collective-permute-done | bytes 196640 | tf_op jit(solution)/shard_map/ppermute | solution.py:212
  17.9 1.3 collective-permute-start.3
  19.2 0.8 copy-done
  20.3 0.8 copy-done.1
  21.4 7.2 %split_history.1 = (bf16[3072,1536]{1,0:T(8,128)(2,1)S(1)}, bf16[3072,1536]{1,0:T(8,128)(2,1)S(1)}) custom-call(f32[24,12,128,128]{3,2,1,0:T(8,128)} %h_hbm.1), custom_call_target="tpu_custom_call" | custom-call | bytes 37748736 | tf_op jit(solution)/shard_map/split_history/pallas_call | solution.py:56
  28.5 2.0 %shard_map.38 = (f32[128,1536]{1,0:T(8,128)S(1)}, bf16[3072,1536]{1,0:T(8,128)(2,1)S(1)}, bf16[3072,1536]{1,0:T(8,128)(2,1)S(1)}) custom-call(f32[2,6,32,128]{3,2,1,0:T(8,128)S(1)} %collective-permute-done.5.refs_0_, f32[2,6,32,128]{3,2,1,0:T(8,128)S(1)} %collective-permute-done.6.refs_1_, ...), custom_call_target="tpu_custom_call", output_to_operand_aliasing={{1}: (4, {}), {2}: (5, {})} | custom-call | flops 1811939328 | bytes 4194304 | tf_op jit(solution)/shard_map/pallas_call | solution.py:158
  30.6 1.1 shard_map.39
  31.8 7.6 %collective-permute-start.10 = (f32[6,32,128]{2,1,0:T(8,128)S(1)}, f32[6,32,128]{2,1,0:T(8,128)S(1)}, u32[]{:S(2)}, u32[]{:S(2)}) collective-permute-start(f32[6,32,128]{2,1,0:T(8,128)S(1)} %get-tuple-element.88), channel_id=1, source_target_pairs={{0,16},{1,17},{2,18},{3,19},{4,20},{5,21},{6,22},{7,23},{8,24},{9,... | collective-permute-start | bytes 294920 | tf_op jit(solution)/shard_map/ppermute | solution.py:212
  39.4 1.5 %collective-permute-start.9 = (f32[6,32,128]{2,1,0:T(8,128)S(1)}, f32[6,32,128]{2,1,0:T(8,128)S(1)}, u32[]{:S(2)}, u32[]{:S(2)}) collective-permute-start(f32[6,32,128]{2,1,0:T(8,128)S(1)} %get-tuple-element.90), channel_id=1, source_target_pairs={{0,8},{1,9},{2,10},{3,11},{4,12},{5,13},{6,14},{7,15},{8,0},{9,1},... | collective-permute-start | bytes 294920 | tf_op jit(solution)/shard_map/ppermute | solution.py:212
  40.9 1.1 shard_map.42
  42.1 2.0 %collective-permute-start.13 = (f32[6,32,128]{2,1,0:T(8,128)S(1)}, f32[6,32,128]{2,1,0:T(8,128)S(1)}, u32[]{:S(2)}, u32[]{:S(2)}) collective-permute-start(f32[6,32,128]{2,1,0:T(8,128)S(1)} %get-tuple-element.85), channel_id=1, source_target_pairs={{0,16},{1,17},{2,18},{3,19},{4,20},{5,21},{6,22},{7,23},{8,24},{9,... | collective-permute-start | bytes 294920 | tf_op jit(solution)/shard_map/ppermute | solution.py:212
  44.6 1.1 collective-permute-start.12
  46.9 1.6 %collective-permute-done.13 = f32[6,32,128]{2,1,0:T(8,128)S(1)} collective-permute-done((f32[6,32,128]{2,1,0:T(8,128)S(1)}, f32[6,32,128]{2,1,0:T(8,128)S(1)}, u32[]{:S(2)}, u32[]{:S(2)}) %collective-permute-start.13) | collective-permute-done | bytes 98336 | tf_op jit(solution)/shard_map/ppermute | solution.py:212
  48.5 2.0 %collective-permute-done.14 = f32[6,32,128]{2,1,0:T(8,128)S(1)} collective-permute-done((f32[6,32,128]{2,1,0:T(8,128)S(1)}, f32[6,32,128]{2,1,0:T(8,128)S(1)}, u32[]{:S(2)}, u32[]{:S(2)}) %collective-permute-start.14) | collective-permute-done | bytes 98336 | tf_op jit(solution)/shard_map/ppermute | solution.py:212
  50.7 4.0 %collective-permute-start.22 = (f32[2,6,32,128]{3,2,1,0:T(8,128)S(1)}, f32[2,6,32,128]{3,2,1,0:T(8,128)S(1)}, u32[]{:S(2)}, u32[]{:S(2)}) collective-permute-start(f32[2,6,32,128]{3,2,1,0:T(8,128)S(1)} %pad_maximum_fusion.3), channel_id=1, source_target_pairs={{0,6},{1,3},{2,14},{3,11},{4,22},{5,19},{6,30},{7,27},{8,4},{9,1},... | collective-permute-start | bytes 589832 | tf_op jit(solution)/shard_map/ppermute | solution.py:212
  55.4 3.5 %collective-permute-start.17 = (f32[2,6,32,128]{3,2,1,0:T(8,128)S(1)}, f32[2,6,32,128]{3,2,1,0:T(8,128)S(1)}, u32[]{:S(2)}, u32[]{:S(2)}) collective-permute-start(f32[2,6,32,128]{3,2,1,0:T(8,128)S(1)} %pad_maximum_fusion.2), channel_id=1, source_target_pairs={{0,6},{1,3},{2,14},{3,11},{4,22},{5,19},{6,30},{7,27},{8,4},{9,1},... | collective-permute-start | bytes 589832 | tf_op jit(solution)/shard_map/ppermute | solution.py:212
  59.6 2.5 %collective-permute-start.24 = (f32[2,6,32,128]{3,2,1,0:T(8,128)S(1)}, f32[2,6,32,128]{3,2,1,0:T(8,128)S(1)}, u32[]{:S(2)}, u32[]{:S(2)}) collective-permute-start(f32[2,6,32,128]{3,2,1,0:T(8,128)S(1)} %collective-permute-done.22.refs_1_), channel_id=1, source_target_pairs={{0,1},{1,0},{2,3},{3,2},{4,5},{5,4},{6,7},{7,6},{8,9},{9,8},{10,11... | collective-permute-start | bytes 589832 | tf_op jit(solution)/shard_map/ppermute | solution.py:212
  62.1 2.1 %collective-permute-done.17.refs_1_ = f32[2,6,32,128]{3,2,1,0:T(8,128)S(1)} collective-permute-done((f32[2,6,32,128]{3,2,1,0:T(8,128)S(1)}, f32[2,6,32,128]{3,2,1,0:T(8,128)S(1)}, u32[]{:S(2)}, u32[]{:S(2)}) %collective-permute-start.17) | collective-permute-done | bytes 196640 | tf_op jit(solution)/shard_map/ppermute | solution.py:212
  64.5 2.0 %collective-permute-start.18 = (f32[2,6,32,128]{3,2,1,0:T(8,128)S(1)}, f32[2,6,32,128]{3,2,1,0:T(8,128)S(1)}, u32[]{:S(2)}, u32[]{:S(2)}) collective-permute-start(f32[2,6,32,128]{3,2,1,0:T(8,128)S(1)} %collective-permute-done.16.refs_0_), channel_id=1, source_target_pairs={{0,1},{1,0},{2,3},{3,2},{4,5},{5,4},{6,7},{7,6},{8,9},{9,8},{10,11... | collective-permute-start | bytes 589832 | tf_op jit(solution)/shard_map/ppermute | solution.py:212
  67.0 2.0 %shard_map.44 = (f32[128,1536]{1,0:T(8,128)S(1)}, bf16[3072,1536]{1,0:T(8,128)(2,1)S(1)}, bf16[3072,1536]{1,0:T(8,128)(2,1)S(1)}) custom-call(f32[2,6,32,128]{3,2,1,0:T(8,128)S(1)} %collective-permute-done.21.refs_0_, f32[2,6,32,128]{3,2,1,0:T(8,128)S(1)} %collective-permute-done.22.refs_1_, ...), custom_call_target="tpu_custom_call", output_to_operand_aliasing={{1}: (4, {}), {2}: (5, {})} | custom-call | flops 1811939328 | bytes 4194304 | tf_op jit(solution)/shard_map/pallas_call | solution.py:158
  69.0 1.1 shard_map.45
  70.2 8.3 %collective-permute-start.26 = (f32[6,32,128]{2,1,0:T(8,128)S(1)}, f32[6,32,128]{2,1,0:T(8,128)S(1)}, u32[]{:S(2)}, u32[]{:S(2)}) collective-permute-start(f32[6,32,128]{2,1,0:T(8,128)S(1)} %get-tuple-element.81), channel_id=1, source_target_pairs={{0,16},{1,17},{2,18},{3,19},{4,20},{5,21},{6,22},{7,23},{8,24},{9,... | collective-permute-start | bytes 294920 | tf_op jit(solution)/shard_map/ppermute | solution.py:212
  78.5 1.5 %collective-permute-start.25 = (f32[6,32,128]{2,1,0:T(8,128)S(1)}, f32[6,32,128]{2,1,0:T(8,128)S(1)}, u32[]{:S(2)}, u32[]{:S(2)}) collective-permute-start(f32[6,32,128]{2,1,0:T(8,128)S(1)} %get-tuple-element.83), channel_id=1, source_target_pairs={{0,8},{1,9},{2,10},{3,11},{4,12},{5,13},{6,14},{7,15},{8,0},{9,1},... | collective-permute-start | bytes 294920 | tf_op jit(solution)/shard_map/ppermute | solution.py:212
  80.0 1.1 shard_map.48
  81.2 2.0 %collective-permute-start.29 = (f32[6,32,128]{2,1,0:T(8,128)S(1)}, f32[6,32,128]{2,1,0:T(8,128)S(1)}, u32[]{:S(2)}, u32[]{:S(2)}) collective-permute-start(f32[6,32,128]{2,1,0:T(8,128)S(1)} %get-tuple-element.78), channel_id=1, source_target_pairs={{0,16},{1,17},{2,18},{3,19},{4,20},{5,21},{6,22},{7,23},{8,24},{9,... | collective-permute-start | bytes 294920 | tf_op jit(solution)/shard_map/ppermute | solution.py:212
  83.7 1.1 collective-permute-start.28
  85.9 1.7 %collective-permute-done.29 = f32[6,32,128]{2,1,0:T(8,128)S(1)} collective-permute-done((f32[6,32,128]{2,1,0:T(8,128)S(1)}, f32[6,32,128]{2,1,0:T(8,128)S(1)}, u32[]{:S(2)}, u32[]{:S(2)}) %collective-permute-start.29) | collective-permute-done | bytes 98336 | tf_op jit(solution)/shard_map/ppermute | solution.py:212
  87.6 2.0 %collective-permute-done.30 = f32[6,32,128]{2,1,0:T(8,128)S(1)} collective-permute-done((f32[6,32,128]{2,1,0:T(8,128)S(1)}, f32[6,32,128]{2,1,0:T(8,128)S(1)}, u32[]{:S(2)}, u32[]{:S(2)}) %collective-permute-start.30) | collective-permute-done | bytes 98336 | tf_op jit(solution)/shard_map/ppermute | solution.py:212
  89.8 3.7 %collective-permute-start.38 = (f32[2,6,32,128]{3,2,1,0:T(8,128)S(1)}, f32[2,6,32,128]{3,2,1,0:T(8,128)S(1)}, u32[]{:S(2)}, u32[]{:S(2)}) collective-permute-start(f32[2,6,32,128]{3,2,1,0:T(8,128)S(1)} %pad_maximum_fusion.5), channel_id=1, source_target_pairs={{0,6},{1,3},{2,14},{3,11},{4,22},{5,19},{6,30},{7,27},{8,4},{9,1},... | collective-permute-start | bytes 589832 | tf_op jit(solution)/shard_map/ppermute | solution.py:212
  94.2 3.8 %collective-permute-start.33 = (f32[2,6,32,128]{3,2,1,0:T(8,128)S(1)}, f32[2,6,32,128]{3,2,1,0:T(8,128)S(1)}, u32[]{:S(2)}, u32[]{:S(2)}) collective-permute-start(f32[2,6,32,128]{3,2,1,0:T(8,128)S(1)} %pad_maximum_fusion.4), channel_id=1, source_target_pairs={{0,6},{1,3},{2,14},{3,11},{4,22},{5,19},{6,30},{7,27},{8,4},{9,1},... | collective-permute-start | bytes 589832 | tf_op jit(solution)/shard_map/ppermute | solution.py:212
  98.0 0.8 collective-permute-start.32
  98.8 2.3 %collective-permute-start.40 = (f32[2,6,32,128]{3,2,1,0:T(8,128)S(1)}, f32[2,6,32,128]{3,2,1,0:T(8,128)S(1)}, u32[]{:S(2)}, u32[]{:S(2)}) collective-permute-start(f32[2,6,32,128]{3,2,1,0:T(8,128)S(1)} %collective-permute-done.38.refs_1_), channel_id=1, source_target_pairs={{0,1},{1,0},{2,3},{3,2},{4,5},{5,4},{6,7},{7,6},{8,9},{9,8},{10,11... | collective-permute-start | bytes 589832 | tf_op jit(solution)/shard_map/ppermute | solution.py:212
  101.2 2.1 %collective-permute-done.33.refs_1_ = f32[2,6,32,128]{3,2,1,0:T(8,128)S(1)} collective-permute-done((f32[2,6,32,128]{3,2,1,0:T(8,128)S(1)}, f32[2,6,32,128]{3,2,1,0:T(8,128)S(1)}, u32[]{:S(2)}, u32[]{:S(2)}) %collective-permute-start.33) | collective-permute-done | bytes 196640 | tf_op jit(solution)/shard_map/ppermute | solution.py:212
  103.3 2.0 %collective-permute-start.34 = (f32[2,6,32,128]{3,2,1,0:T(8,128)S(1)}, f32[2,6,32,128]{3,2,1,0:T(8,128)S(1)}, u32[]{:S(2)}, u32[]{:S(2)}) collective-permute-start(f32[2,6,32,128]{3,2,1,0:T(8,128)S(1)} %collective-permute-done.32.refs_0_), channel_id=1, source_target_pairs={{0,1},{1,0},{2,3},{3,2},{4,5},{5,4},{6,7},{7,6},{8,9},{9,8},{10,11... | collective-permute-start | bytes 589832 | tf_op jit(solution)/shard_map/ppermute | solution.py:212
  105.8 2.0 %shard_map.50 = (f32[128,1536]{1,0:T(8,128)S(1)}, bf16[3072,1536]{1,0:T(8,128)(2,1)S(1)}, bf16[3072,1536]{1,0:T(8,128)(2,1)S(1)}) custom-call(f32[2,6,32,128]{3,2,1,0:T(8,128)S(1)} %collective-permute-done.37.refs_0_, f32[2,6,32,128]{3,2,1,0:T(8,128)S(1)} %collective-permute-done.38.refs_1_, ...), custom_call_target="tpu_custom_call", output_to_operand_aliasing={{1}: (4, {}), {2}: (5, {})} | custom-call | flops 1811939328 | bytes 4194304 | tf_op jit(solution)/shard_map/pallas_call | solution.py:158
  107.8 1.1 shard_map.51
  109.0 8.1 %collective-permute-start.42 = (f32[6,32,128]{2,1,0:T(8,128)S(1)}, f32[6,32,128]{2,1,0:T(8,128)S(1)}, u32[]{:S(2)}, u32[]{:S(2)}) collective-permute-start(f32[6,32,128]{2,1,0:T(8,128)S(1)} %get-tuple-element.74), channel_id=1, source_target_pairs={{0,16},{1,17},{2,18},{3,19},{4,20},{5,21},{6,22},{7,23},{8,24},{9,... | collective-permute-start | bytes 294920 | tf_op jit(solution)/shard_map/ppermute | solution.py:212
  117.1 1.5 %collective-permute-start.41 = (f32[6,32,128]{2,1,0:T(8,128)S(1)}, f32[6,32,128]{2,1,0:T(8,128)S(1)}, u32[]{:S(2)}, u32[]{:S(2)}) collective-permute-start(f32[6,32,128]{2,1,0:T(8,128)S(1)} %get-tuple-element.76), channel_id=1, source_target_pairs={{0,8},{1,9},{2,10},{3,11},{4,12},{5,13},{6,14},{7,15},{8,0},{9,1},... | collective-permute-start | bytes 294920 | tf_op jit(solution)/shard_map/ppermute | solution.py:212
  118.6 1.1 shard_map.54
  119.8 2.0 %collective-permute-start.45 = (f32[6,32,128]{2,1,0:T(8,128)S(1)}, f32[6,32,128]{2,1,0:T(8,128)S(1)}, u32[]{:S(2)}, u32[]{:S(2)}) collective-permute-start(f32[6,32,128]{2,1,0:T(8,128)S(1)} %get-tuple-element.71), channel_id=1, source_target_pairs={{0,16},{1,17},{2,18},{3,19},{4,20},{5,21},{6,22},{7,23},{8,24},{9,... | collective-permute-start | bytes 294920 | tf_op jit(solution)/shard_map/ppermute | solution.py:212
  122.3 1.1 collective-permute-start.44
  124.4 1.8 %collective-permute-done.45 = f32[6,32,128]{2,1,0:T(8,128)S(1)} collective-permute-done((f32[6,32,128]{2,1,0:T(8,128)S(1)}, f32[6,32,128]{2,1,0:T(8,128)S(1)}, u32[]{:S(2)}, u32[]{:S(2)}) %collective-permute-start.45) | collective-permute-done | bytes 98336 | tf_op jit(solution)/shard_map/ppermute | solution.py:212
  126.2 2.0 %collective-permute-done.46 = f32[6,32,128]{2,1,0:T(8,128)S(1)} collective-permute-done((f32[6,32,128]{2,1,0:T(8,128)S(1)}, f32[6,32,128]{2,1,0:T(8,128)S(1)}, u32[]{:S(2)}, u32[]{:S(2)}) %collective-permute-start.46) | collective-permute-done | bytes 98336 | tf_op jit(solution)/shard_map/ppermute | solution.py:212
  128.2 0.8 copy-done.3
  (94 shorter events, 11.3 us)
Async XLA Ops:
  0.0 1.8 %collective-permute-start = (f32[12,32,128]{2,1,0:T(8,128)}, f32[12,32,128]{2,1,0:T(8,128)S(1)}, u32[]{:S(2)}, u32[]{:S(2)}) collective-permute-start(f32[12,32,128]{2,1,0:T(8,128)} %bitcast.94), channel_id=1, source_target_pairs={{0,1},{1,0},{2,3},{3,2},{4,5},{5,4},{6,7},{7,6},{8,9},{9,8},{10,11... | collective-permute-start | bytes 589832 | tf_op jit(solution)/shard_map/ppermute | solution.py:212
  1.8 10.1 %collective-permute-start.6 = (f32[2,6,32,128]{3,2,1,0:T(8,128)S(1)}, f32[2,6,32,128]{3,2,1,0:T(8,128)S(1)}, u32[]{:S(2)}, u32[]{:S(2)}) collective-permute-start(f32[2,6,32,128]{3,2,1,0:T(8,128)S(1)} %pad_maximum_fusion.1), channel_id=1, source_target_pairs={{0,6},{1,3},{2,14},{3,11},{4,22},{5,19},{6,30},{7,27},{8,4},{9,1},... | collective-permute-start | bytes 589832 | tf_op jit(solution)/shard_map/ppermute | solution.py:212
  6.8 7.1 %collective-permute-start.5 = (f32[2,6,32,128]{3,2,1,0:T(8,128)S(1)}, f32[2,6,32,128]{3,2,1,0:T(8,128)S(1)}, u32[]{:S(2)}, u32[]{:S(2)}) collective-permute-start(f32[2,6,32,128]{3,2,1,0:T(8,128)S(1)} %pad_maximum_fusion.1), channel_id=1, source_target_pairs={{0,0},{1,5},{2,8},{3,13},{4,16},{5,21},{6,24},{7,29},{8,2},{9,7},{... | collective-permute-start | bytes 589832 | tf_op jit(solution)/shard_map/ppermute | solution.py:212
  7.5 10.4 %collective-permute-start.2 = (f32[2,6,32,128]{3,2,1,0:T(8,128)S(1)}, f32[2,6,32,128]{3,2,1,0:T(8,128)S(1)}, u32[]{:S(2)}, u32[]{:S(2)}) collective-permute-start(f32[2,6,32,128]{3,2,1,0:T(8,128)S(1)} %pad_maximum_fusion), channel_id=1, source_target_pairs={{0,6},{1,3},{2,14},{3,11},{4,22},{5,19},{6,30},{7,27},{8,4},{9,1},... | collective-permute-start | bytes 589832 | tf_op jit(solution)/shard_map/ppermute | solution.py:212
  11.3 6.7 %collective-permute-start.1 = (f32[2,6,32,128]{3,2,1,0:T(8,128)S(1)}, f32[2,6,32,128]{3,2,1,0:T(8,128)S(1)}, u32[]{:S(2)}, u32[]{:S(2)}) collective-permute-start(f32[2,6,32,128]{3,2,1,0:T(8,128)S(1)} %pad_maximum_fusion), channel_id=1, source_target_pairs={{0,0},{1,5},{2,8},{3,13},{4,16},{5,21},{6,24},{7,29},{8,2},{9,7},{... | collective-permute-start | bytes 589832 | tf_op jit(solution)/shard_map/ppermute | solution.py:212
  11.9 16.6 %collective-permute-start.8 = (f32[2,6,32,128]{3,2,1,0:T(8,128)S(1)}, f32[2,6,32,128]{3,2,1,0:T(8,128)S(1)}, u32[]{:S(2)}, u32[]{:S(2)}) collective-permute-start(f32[2,6,32,128]{3,2,1,0:T(8,128)S(1)} %collective-permute-done.6.refs_1_), channel_id=1, source_target_pairs={{0,1},{1,0},{2,3},{3,2},{4,5},{5,4},{6,7},{7,6},{8,9},{9,8},{10,11... | collective-permute-start | bytes 589832 | tf_op jit(solution)/shard_map/ppermute | solution.py:212
  14.0 14.6 %collective-permute-start.7 = (f32[2,6,32,128]{3,2,1,0:T(8,128)S(1)}, f32[2,6,32,128]{3,2,1,0:T(8,128)S(1)}, u32[]{:S(2)}, u32[]{:S(2)}) collective-permute-start(f32[2,6,32,128]{3,2,1,0:T(8,128)S(1)} %collective-permute-done.5.refs_0_), channel_id=1, source_target_pairs={{0,1},{1,0},{2,3},{3,2},{4,5},{5,4},{6,7},{7,6},{8,9},{9,8},{10,11... | collective-permute-start | bytes 589832 | tf_op jit(solution)/shard_map/ppermute | solution.py:212
  17.9 12.6 %collective-permute-start.4 = (f32[2,6,32,128]{3,2,1,0:T(8,128)S(1)}, f32[2,6,32,128]{3,2,1,0:T(8,128)S(1)}, u32[]{:S(2)}, u32[]{:S(2)}) collective-permute-start(f32[2,6,32,128]{3,2,1,0:T(8,128)S(1)} %collective-permute-done.2.refs_1_), channel_id=1, source_target_pairs={{0,1},{1,0},{2,3},{3,2},{4,5},{5,4},{6,7},{7,6},{8,9},{9,8},{10,11... | collective-permute-start | bytes 589832 | tf_op jit(solution)/shard_map/ppermute | solution.py:212
  17.9 12.6 %collective-permute-start.3 = (f32[2,6,32,128]{3,2,1,0:T(8,128)S(1)}, f32[2,6,32,128]{3,2,1,0:T(8,128)S(1)}, u32[]{:S(2)}, u32[]{:S(2)}) collective-permute-start(f32[2,6,32,128]{3,2,1,0:T(8,128)S(1)} %collective-permute-done.1.refs_0_), channel_id=1, source_target_pairs={{0,1},{1,0},{2,3},{3,2},{4,5},{5,4},{6,7},{7,6},{8,9},{9,8},{10,11... | collective-permute-start | bytes 589832 | tf_op jit(solution)/shard_map/ppermute | solution.py:212
  31.8 12.8 %collective-permute-start.10 = (f32[6,32,128]{2,1,0:T(8,128)S(1)}, f32[6,32,128]{2,1,0:T(8,128)S(1)}, u32[]{:S(2)}, u32[]{:S(2)}) collective-permute-start(f32[6,32,128]{2,1,0:T(8,128)S(1)} %get-tuple-element.88), channel_id=1, source_target_pairs={{0,16},{1,17},{2,18},{3,19},{4,20},{5,21},{6,22},{7,23},{8,24},{9,... | collective-permute-start | bytes 294920 | tf_op jit(solution)/shard_map/ppermute | solution.py:212
  39.4 6.6 %collective-permute-start.11 = (f32[6,32,128]{2,1,0:T(8,128)S(1)}, f32[6,32,128]{2,1,0:T(8,128)S(1)}, u32[]{:S(2)}, u32[]{:S(2)}) collective-permute-start(f32[6,32,128]{2,1,0:T(8,128)S(1)} %get-tuple-element.89), channel_id=1, source_target_pairs={{0,24},{1,25},{2,26},{3,27},{4,28},{5,29},{6,30},{7,31},{8,16},{9,... | collective-permute-start | bytes 294920 | tf_op jit(solution)/shard_map/ppermute | solution.py:212
  39.4 7.3 %collective-permute-start.9 = (f32[6,32,128]{2,1,0:T(8,128)S(1)}, f32[6,32,128]{2,1,0:T(8,128)S(1)}, u32[]{:S(2)}, u32[]{:S(2)}) collective-permute-start(f32[6,32,128]{2,1,0:T(8,128)S(1)} %get-tuple-element.90), channel_id=1, source_target_pairs={{0,8},{1,9},{2,10},{3,11},{4,12},{5,13},{6,14},{7,15},{8,0},{9,1},... | collective-permute-start | bytes 294920 | tf_op jit(solution)/shard_map/ppermute | solution.py:212
  40.9 25.5 %copy-start.2 = (f32[128,128]{1,0:T(8,128)S(1)}, f32[128,128]{1,0:T(8,128)}, u32[]{:S(2)}) copy-start(f32[128,128]{1,0:T(8,128)} %hamiltonian.11) | copy-start | bytes 196612
  42.1 6.4 %collective-permute-start.13 = (f32[6,32,128]{2,1,0:T(8,128)S(1)}, f32[6,32,128]{2,1,0:T(8,128)S(1)}, u32[]{:S(2)}, u32[]{:S(2)}) collective-permute-start(f32[6,32,128]{2,1,0:T(8,128)S(1)} %get-tuple-element.85), channel_id=1, source_target_pairs={{0,16},{1,17},{2,18},{3,19},{4,20},{5,21},{6,22},{7,23},{8,24},{9,... | collective-permute-start | bytes 294920 | tf_op jit(solution)/shard_map/ppermute | solution.py:212
  44.1 6.4 %collective-permute-start.14 = (f32[6,32,128]{2,1,0:T(8,128)S(1)}, f32[6,32,128]{2,1,0:T(8,128)S(1)}, u32[]{:S(2)}, u32[]{:S(2)}) collective-permute-start(f32[6,32,128]{2,1,0:T(8,128)S(1)} %get-tuple-element.86), channel_id=1, source_target_pairs={{0,24},{1,25},{2,26},{3,27},{4,28},{5,29},{6,30},{7,31},{8,16},{9,... | collective-permute-start | bytes 294920 | tf_op jit(solution)/shard_map/ppermute | solution.py:212
  44.6 5.9 %collective-permute-start.12 = (f32[6,32,128]{2,1,0:T(8,128)S(1)}, f32[6,32,128]{2,1,0:T(8,128)S(1)}, u32[]{:S(2)}, u32[]{:S(2)}) collective-permute-start(f32[6,32,128]{2,1,0:T(8,128)S(1)} %get-tuple-element.87), channel_id=1, source_target_pairs={{0,8},{1,9},{2,10},{3,11},{4,12},{5,13},{6,14},{7,15},{8,0},{9,1},... | collective-permute-start | bytes 294920 | tf_op jit(solution)/shard_map/ppermute | solution.py:212
  46.7 3.9 %collective-permute-start.20 = (f32[6,32,128]{2,1,0:T(8,128)S(1)}, f32[6,32,128]{2,1,0:T(8,128)S(1)}, u32[]{:S(2)}, u32[]{:S(2)}) collective-permute-start(f32[6,32,128]{2,1,0:T(8,128)S(1)} %multiply_subtract_fusion.1.value), channel_id=1, source_target_pairs={{0,1},{1,0},{2,3},{3,2},{4,5},{5,4},{6,7},{7,6},{8,9},{9,8},{10,11... | collective-permute-start | bytes 294920 | tf_op jit(solution)/shard_map/ppermute | solution.py:212
  50.6 4.8 %collective-permute-start.15 = (f32[6,32,128]{2,1,0:T(8,128)S(1)}, f32[6,32,128]{2,1,0:T(8,128)S(1)}, u32[]{:S(2)}, u32[]{:S(2)}) collective-permute-start(f32[6,32,128]{2,1,0:T(8,128)S(1)} %get-tuple-element.70.value), channel_id=1, source_target_pairs={{0,1},{1,0},{2,3},{3,2},{4,5},{5,4},{6,7},{7,6},{8,9},{9,8},{10,11... | collective-permute-start | bytes 294920 | tf_op jit(solution)/shard_map/ppermute | solution.py:212
  50.7 8.9 %collective-permute-start.22 = (f32[2,6,32,128]{3,2,1,0:T(8,128)S(1)}, f32[2,6,32,128]{3,2,1,0:T(8,128)S(1)}, u32[]{:S(2)}, u32[]{:S(2)}) collective-permute-start(f32[2,6,32,128]{3,2,1,0:T(8,128)S(1)} %pad_maximum_fusion.3), channel_id=1, source_target_pairs={{0,6},{1,3},{2,14},{3,11},{4,22},{5,19},{6,30},{7,27},{8,4},{9,1},... | collective-permute-start | bytes 589832 | tf_op jit(solution)/shard_map/ppermute | solution.py:212
  54.7 7.4 %collective-permute-start.21 = (f32[2,6,32,128]{3,2,1,0:T(8,128)S(1)}, f32[2,6,32,128]{3,2,1,0:T(8,128)S(1)}, u32[]{:S(2)}, u32[]{:S(2)}) collective-permute-start(f32[2,6,32,128]{3,2,1,0:T(8,128)S(1)} %pad_maximum_fusion.3), channel_id=1, source_target_pairs={{0,0},{1,5},{2,8},{3,13},{4,16},{5,21},{6,24},{7,29},{8,2},{9,7},{... | collective-permute-start | bytes 589832 | tf_op jit(solution)/shard_map/ppermute | solution.py:212
  55.4 8.8 %collective-permute-start.17 = (f32[2,6,32,128]{3,2,1,0:T(8,128)S(1)}, f32[2,6,32,128]{3,2,1,0:T(8,128)S(1)}, u32[]{:S(2)}, u32[]{:S(2)}) collective-permute-start(f32[2,6,32,128]{3,2,1,0:T(8,128)S(1)} %pad_maximum_fusion.2), channel_id=1, source_target_pairs={{0,6},{1,3},{2,14},{3,11},{4,22},{5,19},{6,30},{7,27},{8,4},{9,1},... | collective-permute-start | bytes 589832 | tf_op jit(solution)/shard_map/ppermute | solution.py:212
  58.9 5.6 %collective-permute-start.16 = (f32[2,6,32,128]{3,2,1,0:T(8,128)S(1)}, f32[2,6,32,128]{3,2,1,0:T(8,128)S(1)}, u32[]{:S(2)}, u32[]{:S(2)}) collective-permute-start(f32[2,6,32,128]{3,2,1,0:T(8,128)S(1)} %pad_maximum_fusion.2), channel_id=1, source_target_pairs={{0,0},{1,5},{2,8},{3,13},{4,16},{5,21},{6,24},{7,29},{8,2},{9,7},{... | collective-permute-start | bytes 589832 | tf_op jit(solution)/shard_map/ppermute | solution.py:212
  59.6 7.4 %collective-permute-start.24 = (f32[2,6,32,128]{3,2,1,0:T(8,128)S(1)}, f32[2,6,32,128]{3,2,1,0:T(8,128)S(1)}, u32[]{:S(2)}, u32[]{:S(2)}) collective-permute-start(f32[2,6,32,128]{3,2,1,0:T(8,128)S(1)} %collective-permute-done.22.refs_1_), channel_id=1, source_target_pairs={{0,1},{1,0},{2,3},{3,2},{4,5},{5,4},{6,7},{7,6},{8,9},{9,8},{10,11... | collective-permute-start | bytes 589832 | tf_op jit(solution)/shard_map/ppermute | solution.py:212
  62.0 4.9 %collective-permute-start.23 = (f32[2,6,32,128]{3,2,1,0:T(8,128)S(1)}, f32[2,6,32,128]{3,2,1,0:T(8,128)S(1)}, u32[]{:S(2)}, u32[]{:S(2)}) collective-permute-start(f32[2,6,32,128]{3,2,1,0:T(8,128)S(1)} %collective-permute-done.21.refs_0_), channel_id=1, source_target_pairs={{0,1},{1,0},{2,3},{3,2},{4,5},{5,4},{6,7},{7,6},{8,9},{9,8},{10,11... | collective-permute-start | bytes 589832 | tf_op jit(solution)/shard_map/ppermute | solution.py:212
  64.2 4.8 %collective-permute-start.19 = (f32[2,6,32,128]{3,2,1,0:T(8,128)S(1)}, f32[2,6,32,128]{3,2,1,0:T(8,128)S(1)}, u32[]{:S(2)}, u32[]{:S(2)}) collective-permute-start(f32[2,6,32,128]{3,2,1,0:T(8,128)S(1)} %collective-permute-done.17.refs_1_), channel_id=1, source_target_pairs={{0,1},{1,0},{2,3},{3,2},{4,5},{5,4},{6,7},{7,6},{8,9},{9,8},{10,11... | collective-permute-start | bytes 589832 | tf_op jit(solution)/shard_map/ppermute | solution.py:212
  64.5 4.6 %collective-permute-start.18 = (f32[2,6,32,128]{3,2,1,0:T(8,128)S(1)}, f32[2,6,32,128]{3,2,1,0:T(8,128)S(1)}, u32[]{:S(2)}, u32[]{:S(2)}) collective-permute-start(f32[2,6,32,128]{3,2,1,0:T(8,128)S(1)} %collective-permute-done.16.refs_0_), channel_id=1, source_target_pairs={{0,1},{1,0},{2,3},{3,2},{4,5},{5,4},{6,7},{7,6},{8,9},{9,8},{10,11... | collective-permute-start | bytes 589832 | tf_op jit(solution)/shard_map/ppermute | solution.py:212
  70.2 13.5 %collective-permute-start.26 = (f32[6,32,128]{2,1,0:T(8,128)S(1)}, f32[6,32,128]{2,1,0:T(8,128)S(1)}, u32[]{:S(2)}, u32[]{:S(2)}) collective-permute-start(f32[6,32,128]{2,1,0:T(8,128)S(1)} %get-tuple-element.81), channel_id=1, source_target_pairs={{0,16},{1,17},{2,18},{3,19},{4,20},{5,21},{6,22},{7,23},{8,24},{9,... | collective-permute-start | bytes 294920 | tf_op jit(solution)/shard_map/ppermute | solution.py:212
  78.5 6.6 %collective-permute-start.27 = (f32[6,32,128]{2,1,0:T(8,128)S(1)}, f32[6,32,128]{2,1,0:T(8,128)S(1)}, u32[]{:S(2)}, u32[]{:S(2)}) collective-permute-start(f32[6,32,128]{2,1,0:T(8,128)S(1)} %get-tuple-element.82), channel_id=1, source_target_pairs={{0,24},{1,25},{2,26},{3,27},{4,28},{5,29},{6,30},{7,31},{8,16},{9,... | collective-permute-start | bytes 294920 | tf_op jit(solution)/shard_map/ppermute | solution.py:212
  78.5 7.3 %collective-permute-start.25 = (f32[6,32,128]{2,1,0:T(8,128)S(1)}, f32[6,32,128]{2,1,0:T(8,128)S(1)}, u32[]{:S(2)}, u32[]{:S(2)}) collective-permute-start(f32[6,32,128]{2,1,0:T(8,128)S(1)} %get-tuple-element.83), channel_id=1, source_target_pairs={{0,8},{1,9},{2,10},{3,11},{4,12},{5,13},{6,14},{7,15},{8,0},{9,1},... | collective-permute-start | bytes 294920 | tf_op jit(solution)/shard_map/ppermute | solution.py:212
  81.2 6.4 %collective-permute-start.29 = (f32[6,32,128]{2,1,0:T(8,128)S(1)}, f32[6,32,128]{2,1,0:T(8,128)S(1)}, u32[]{:S(2)}, u32[]{:S(2)}) collective-permute-start(f32[6,32,128]{2,1,0:T(8,128)S(1)} %get-tuple-element.78), channel_id=1, source_target_pairs={{0,16},{1,17},{2,18},{3,19},{4,20},{5,21},{6,22},{7,23},{8,24},{9,... | collective-permute-start | bytes 294920 | tf_op jit(solution)/shard_map/ppermute | solution.py:212
  83.2 6.4 %collective-permute-start.30 = (f32[6,32,128]{2,1,0:T(8,128)S(1)}, f32[6,32,128]{2,1,0:T(8,128)S(1)}, u32[]{:S(2)}, u32[]{:S(2)}) collective-permute-start(f32[6,32,128]{2,1,0:T(8,128)S(1)} %get-tuple-element.79), channel_id=1, source_target_pairs={{0,24},{1,25},{2,26},{3,27},{4,28},{5,29},{6,30},{7,31},{8,16},{9,... | collective-permute-start | bytes 294920 | tf_op jit(solution)/shard_map/ppermute | solution.py:212
  83.7 5.9 %collective-permute-start.28 = (f32[6,32,128]{2,1,0:T(8,128)S(1)}, f32[6,32,128]{2,1,0:T(8,128)S(1)}, u32[]{:S(2)}, u32[]{:S(2)}) collective-permute-start(f32[6,32,128]{2,1,0:T(8,128)S(1)} %get-tuple-element.80), channel_id=1, source_target_pairs={{0,8},{1,9},{2,10},{3,11},{4,12},{5,13},{6,14},{7,15},{8,0},{9,1},... | collective-permute-start | bytes 294920 | tf_op jit(solution)/shard_map/ppermute | solution.py:212
  85.8 3.9 %collective-permute-start.36 = (f32[6,32,128]{2,1,0:T(8,128)S(1)}, f32[6,32,128]{2,1,0:T(8,128)S(1)}, u32[]{:S(2)}, u32[]{:S(2)}) collective-permute-start(f32[6,32,128]{2,1,0:T(8,128)S(1)} %get-tuple-element.68.value), channel_id=1, source_target_pairs={{0,1},{1,0},{2,3},{3,2},{4,5},{5,4},{6,7},{7,6},{8,9},{9,8},{10,11... | collective-permute-start | bytes 294920 | tf_op jit(solution)/shard_map/ppermute | solution.py:212
  89.6 4.5 %collective-permute-start.31 = (f32[6,32,128]{2,1,0:T(8,128)S(1)}, f32[6,32,128]{2,1,0:T(8,128)S(1)}, u32[]{:S(2)}, u32[]{:S(2)}) collective-permute-start(f32[6,32,128]{2,1,0:T(8,128)S(1)} %get-tuple-element.66.value), channel_id=1, source_target_pairs={{0,1},{1,0},{2,3},{3,2},{4,5},{5,4},{6,7},{7,6},{8,9},{9,8},{10,11... | collective-permute-start | bytes 294920 | tf_op jit(solution)/shard_map/ppermute | solution.py:212
  89.8 9.1 %collective-permute-start.38 = (f32[2,6,32,128]{3,2,1,0:T(8,128)S(1)}, f32[2,6,32,128]{3,2,1,0:T(8,128)S(1)}, u32[]{:S(2)}, u32[]{:S(2)}) collective-permute-start(f32[2,6,32,128]{3,2,1,0:T(8,128)S(1)} %pad_maximum_fusion.5), channel_id=1, source_target_pairs={{0,6},{1,3},{2,14},{3,11},{4,22},{5,19},{6,30},{7,27},{8,4},{9,1},... | collective-permute-start | bytes 589832 | tf_op jit(solution)/shard_map/ppermute | solution.py:212
  93.5 7.6 %collective-permute-start.37 = (f32[2,6,32,128]{3,2,1,0:T(8,128)S(1)}, f32[2,6,32,128]{3,2,1,0:T(8,128)S(1)}, u32[]{:S(2)}, u32[]{:S(2)}) collective-permute-start(f32[2,6,32,128]{3,2,1,0:T(8,128)S(1)} %pad_maximum_fusion.5), channel_id=1, source_target_pairs={{0,0},{1,5},{2,8},{3,13},{4,16},{5,21},{6,24},{7,29},{8,2},{9,7},{... | collective-permute-start | bytes 589832 | tf_op jit(solution)/shard_map/ppermute | solution.py:212
  94.2 9.1 %collective-permute-start.33 = (f32[2,6,32,128]{3,2,1,0:T(8,128)S(1)}, f32[2,6,32,128]{3,2,1,0:T(8,128)S(1)}, u32[]{:S(2)}, u32[]{:S(2)}) collective-permute-start(f32[2,6,32,128]{3,2,1,0:T(8,128)S(1)} %pad_maximum_fusion.4), channel_id=1, source_target_pairs={{0,6},{1,3},{2,14},{3,11},{4,22},{5,19},{6,30},{7,27},{8,4},{9,1},... | collective-permute-start | bytes 589832 | tf_op jit(solution)/shard_map/ppermute | solution.py:212
  98.0 5.3 %collective-permute-start.32 = (f32[2,6,32,128]{3,2,1,0:T(8,128)S(1)}, f32[2,6,32,128]{3,2,1,0:T(8,128)S(1)}, u32[]{:S(2)}, u32[]{:S(2)}) collective-permute-start(f32[2,6,32,128]{3,2,1,0:T(8,128)S(1)} %pad_maximum_fusion.4), channel_id=1, source_target_pairs={{0,0},{1,5},{2,8},{3,13},{4,16},{5,21},{6,24},{7,29},{8,2},{9,7},{... | collective-permute-start | bytes 589832 | tf_op jit(solution)/shard_map/ppermute | solution.py:212
  98.8 6.9 %collective-permute-start.40 = (f32[2,6,32,128]{3,2,1,0:T(8,128)S(1)}, f32[2,6,32,128]{3,2,1,0:T(8,128)S(1)}, u32[]{:S(2)}, u32[]{:S(2)}) collective-permute-start(f32[2,6,32,128]{3,2,1,0:T(8,128)S(1)} %collective-permute-done.38.refs_1_), channel_id=1, source_target_pairs={{0,1},{1,0},{2,3},{3,2},{4,5},{5,4},{6,7},{7,6},{8,9},{9,8},{10,11... | collective-permute-start | bytes 589832 | tf_op jit(solution)/shard_map/ppermute | solution.py:212
  101.1 4.7 %collective-permute-start.39 = (f32[2,6,32,128]{3,2,1,0:T(8,128)S(1)}, f32[2,6,32,128]{3,2,1,0:T(8,128)S(1)}, u32[]{:S(2)}, u32[]{:S(2)}) collective-permute-start(f32[2,6,32,128]{3,2,1,0:T(8,128)S(1)} %collective-permute-done.37.refs_0_), channel_id=1, source_target_pairs={{0,1},{1,0},{2,3},{3,2},{4,5},{5,4},{6,7},{7,6},{8,9},{9,8},{10,11... | collective-permute-start | bytes 589832 | tf_op jit(solution)/shard_map/ppermute | solution.py:212
  103.3 4.5 %collective-permute-start.35 = (f32[2,6,32,128]{3,2,1,0:T(8,128)S(1)}, f32[2,6,32,128]{3,2,1,0:T(8,128)S(1)}, u32[]{:S(2)}, u32[]{:S(2)}) collective-permute-start(f32[2,6,32,128]{3,2,1,0:T(8,128)S(1)} %collective-permute-done.33.refs_1_), channel_id=1, source_target_pairs={{0,1},{1,0},{2,3},{3,2},{4,5},{5,4},{6,7},{7,6},{8,9},{9,8},{10,11... | collective-permute-start | bytes 589832 | tf_op jit(solution)/shard_map/ppermute | solution.py:212
  103.3 4.5 %collective-permute-start.34 = (f32[2,6,32,128]{3,2,1,0:T(8,128)S(1)}, f32[2,6,32,128]{3,2,1,0:T(8,128)S(1)}, u32[]{:S(2)}, u32[]{:S(2)}) collective-permute-start(f32[2,6,32,128]{3,2,1,0:T(8,128)S(1)} %collective-permute-done.32.refs_0_), channel_id=1, source_target_pairs={{0,1},{1,0},{2,3},{3,2},{4,5},{5,4},{6,7},{7,6},{8,9},{9,8},{10,11... | collective-permute-start | bytes 589832 | tf_op jit(solution)/shard_map/ppermute | solution.py:212
  109.0 13.3 %collective-permute-start.42 = (f32[6,32,128]{2,1,0:T(8,128)S(1)}, f32[6,32,128]{2,1,0:T(8,128)S(1)}, u32[]{:S(2)}, u32[]{:S(2)}) collective-permute-start(f32[6,32,128]{2,1,0:T(8,128)S(1)} %get-tuple-element.74), channel_id=1, source_target_pairs={{0,16},{1,17},{2,18},{3,19},{4,20},{5,21},{6,22},{7,23},{8,24},{9,... | collective-permute-start | bytes 294920 | tf_op jit(solution)/shard_map/ppermute | solution.py:212
  117.1 6.6 %collective-permute-start.43 = (f32[6,32,128]{2,1,0:T(8,128)S(1)}, f32[6,32,128]{2,1,0:T(8,128)S(1)}, u32[]{:S(2)}, u32[]{:S(2)}) collective-permute-start(f32[6,32,128]{2,1,0:T(8,128)S(1)} %get-tuple-element.75), channel_id=1, source_target_pairs={{0,24},{1,25},{2,26},{3,27},{4,28},{5,29},{6,30},{7,31},{8,16},{9,... | collective-permute-start | bytes 294920 | tf_op jit(solution)/shard_map/ppermute | solution.py:212
  117.1 7.3 %collective-permute-start.41 = (f32[6,32,128]{2,1,0:T(8,128)S(1)}, f32[6,32,128]{2,1,0:T(8,128)S(1)}, u32[]{:S(2)}, u32[]{:S(2)}) collective-permute-start(f32[6,32,128]{2,1,0:T(8,128)S(1)} %get-tuple-element.76), channel_id=1, source_target_pairs={{0,8},{1,9},{2,10},{3,11},{4,12},{5,13},{6,14},{7,15},{8,0},{9,1},... | collective-permute-start | bytes 294920 | tf_op jit(solution)/shard_map/ppermute | solution.py:212
  119.8 6.4 %collective-permute-start.45 = (f32[6,32,128]{2,1,0:T(8,128)S(1)}, f32[6,32,128]{2,1,0:T(8,128)S(1)}, u32[]{:S(2)}, u32[]{:S(2)}) collective-permute-start(f32[6,32,128]{2,1,0:T(8,128)S(1)} %get-tuple-element.71), channel_id=1, source_target_pairs={{0,16},{1,17},{2,18},{3,19},{4,20},{5,21},{6,22},{7,23},{8,24},{9,... | collective-permute-start | bytes 294920 | tf_op jit(solution)/shard_map/ppermute | solution.py:212
  121.8 6.4 %collective-permute-start.46 = (f32[6,32,128]{2,1,0:T(8,128)S(1)}, f32[6,32,128]{2,1,0:T(8,128)S(1)}, u32[]{:S(2)}, u32[]{:S(2)}) collective-permute-start(f32[6,32,128]{2,1,0:T(8,128)S(1)} %get-tuple-element.72), channel_id=1, source_target_pairs={{0,24},{1,25},{2,26},{3,27},{4,28},{5,29},{6,30},{7,31},{8,16},{9,... | collective-permute-start | bytes 294920 | tf_op jit(solution)/shard_map/ppermute | solution.py:212
  122.3 5.9 %collective-permute-start.44 = (f32[6,32,128]{2,1,0:T(8,128)S(1)}, f32[6,32,128]{2,1,0:T(8,128)S(1)}, u32[]{:S(2)}, u32[]{:S(2)}) collective-permute-start(f32[6,32,128]{2,1,0:T(8,128)S(1)} %get-tuple-element.73), channel_id=1, source_target_pairs={{0,8},{1,9},{2,10},{3,11},{4,12},{5,13},{6,14},{7,15},{8,0},{9,1},... | collective-permute-start | bytes 294920 | tf_op jit(solution)/shard_map/ppermute | solution.py:212
  (3 other events, 2.5 us)
where the time goes:
time: 129 us
  starting transfers between devices  79.4 us (62%)
  waiting for transfers between devices  23.8 us (18%)
  Pallas kernels  21.3 us (17%)
  local copies, waits for them, and re-layouts  3.68 us (3%)
    ppermute x47, starting transfers between devices, move(): return lax.ppermute(value, AXES, pairs(nrow, ncol, target))  79.4 us
    ppermute x47, waiting for transfers between devices, move(): return lax.ppermute(value, AXES, pairs(nrow, ncol, target))  23.8 us
    pallas_call x9, Pallas kernels, call(): pl.pallas_call(kernel, in_specs=[pl.BlockSpec(memory_space=VMEM)] * (coun...  12.7 us
    pallas_call x1, Pallas kernels, split_history(): pl.pallas_call(functools.partial(split_kernel, slots), in_specs=[pl.Block...  7.15 us
  transfers between devices with their start and end apart: 47, of which 19 were waited for; matrix products, arithmetic and copies ran while one was open for 1% of the time, Pallas kernels for 14%

commit v1 on v0

--- a/solution.py
+++ b/solution.py
@@ -20,7 +20,6 @@
 
 def split_kernel(slots, h_hbm, hi_ref, lo_ref, buf, sem):
     times, cols, depth, width = h_hbm.shape
-    piece = cols // CHUNKS
 
     def copy(s):
         return pltpu.make_async_copy(h_hbm.at[s], buf.at[s % slots], sem.at[s % slots])
@@ -34,9 +33,7 @@
             copy(s + slots - 1).start()
 
         copy(s).wait()
-        half, t = s // cols, s % cols
-        order = ((t // piece) * CORES + half) * piece + t % piece
-        rows = pl.ds(pl.multiple_of(order * depth, depth), depth)
+        rows = pl.ds(pl.multiple_of(s * depth, depth), depth)
         for t in range(cols):
             tile = buf[s % slots, t]
             high = tile.astype(jnp.bfloat16)
@@ -100,15 +97,6 @@
                 ).astype(jnp.bfloat16)
 
 
-def product(sig, hi, lo, inner, at):
-    total = sig.shape[0] // 2
-    both = jnp.dot(sig[...], hi[inner, at], preferred_element_type=jnp.float32)
-    rest = jnp.dot(
-        sig[0:total, :], lo[inner, at], preferred_element_type=jnp.float32
-    )
-    return both[0:total] + both[total:] + rest
-
-
 def spread(turns, value, out, t0, group):
     r, m, k = position()
     rows, width = out.shape[2:]
@@ -119,38 +107,20 @@
             ]
 
 
-def first_kernel(turns, panels, *refs):
+def contract_kernel(turns, panels, *refs):
     blocks = refs[:panels]
-    hi, lo, acc, _, _, sig = refs[panels:]
+    hi, lo, out, _, _, sig = refs[panels:]
     fill(turns, blocks, sig)
-    inner = slice(0, sig.shape[1])
-    step = 256
-    for n in range(0, acc.shape[1], step):
-        at = slice(n, n + step)
-        acc[:, at] = product(sig, hi, lo, inner, at)
-
-
-def second_kernel(turns, panels, *refs):
-    blocks = refs[:panels]
-    acc, hi, lo, out, sig, _, _ = refs[panels:]
-    fill(turns, blocks, sig)
-    finish(turns, 0, sig, acc, hi, lo, out)
-
-
-def third_kernel(turns, sig, acc, hi, lo, out, hi_out, lo_out):
-    finish(turns, 1, sig, acc, hi, lo, out)
-
-
-def finish(turns, chunk, sig, acc, hi, lo, out):
-    depth = sig.shape[1]
-    inner = slice(depth, 2 * depth)
+    total = sig.shape[0] // 2
     cols, _, width = out.shape[1:]
-    group = 2
+    group = 4 if cols % 4 == 0 else 1
     for t0 in range(0, cols, group):
-        n = (chunk * cols + t0) * width
-        at = slice(n, n + group * width)
-        value = acc[:, at] + product(sig, hi, lo, inner, at)
-        spread(turns, value, out, t0, group)
+        at = slice(t0 * width, (t0 + group) * width)
+        both = jnp.dot(sig[...], hi[:, at], preferred_element_type=jnp.float32)
+        rest = jnp.dot(
+            sig[0:total, :], lo[:, at], preferred_element_type=jnp.float32
+        )
+        spread(turns, both[0:total] + both[total:] + rest, out, t0, group)
 
 
 def call(kernel, inputs, hi, lo, outs, scratch, flops):
@@ -214,9 +184,7 @@
     def partner(value):
         return move(value, lambda r, m, k: (r, m * CORES + 1 - k))
 
-    turns = []
-    for d in range(nrow // 4):
-        turns += [(d, d ^ nrow // 2), (d ^ nrow - 1, d ^ nrow // 2 ^ nrow - 1)]
+    turns = [(nrow - 1 - d, d) for d in range(nrow // CORES)]
     sends = [
         lambda r, m, k, turn=turn: (m, (r ^ turn[k]) * CORES + k) for turn in turns
     ]
@@ -227,7 +195,7 @@
         return mine + [partner(block) for block in mine]
 
     def reduce(parts):
-        return [parts[0]] + [
+        return [
             move(parts[x], lambda r, m, k, x=x: (r ^ x, m * CORES + k))
             for x in range(1, nrow)
         ]
@@ -235,46 +203,31 @@
     hi, lo = split_history(history)
     start = jnp.transpose(new_row, (1, 0, 2))
     cols, rows, width = start.shape
-    piece = cols // CHUNKS
+    piece = rows // CHUNKS
     swapped = partner(start)
-    state = [start[a * piece : (a + 1) * piece] for a in range(CHUNKS)]
-    other = [swapped[a * piece : (a + 1) * piece] for a in range(CHUNKS)]
-    total = nrow * rows
-    depth = hi.shape[0] // CHUNKS
-    part = jax.ShapeDtypeStruct((nrow, piece, rows, width), jnp.float32)
-    acc_type = jax.ShapeDtypeStruct((total, hi.shape[1]), jnp.float32)
-    sig_type = jax.ShapeDtypeStruct((2 * total, depth), jnp.bfloat16)
-    flops = 3 * total * depth * hi.shape[1]
+    state = [start[:, a * piece : (a + 1) * piece] for a in range(CHUNKS)]
+    other = [swapped[:, a * piece : (a + 1) * piece] for a in range(CHUNKS)]
+    total = nrow * piece
+    inner, outer = hi.shape
+    parts_type = jax.ShapeDtypeStruct((nrow, cols, piece, width), jnp.float32)
     rows_out = jnp.zeros((STEPS, cols, rows, width), jnp.float32)
     for n in range(STEPS):
-        if n > 0:
-            other = [partner(state[a]) for a in range(CHUNKS)]
-        blocks = [gather(state[a], other[a]) for a in range(CHUNKS)]
-        base = []
-        for value in state:
-            base.append(small_call(base_kernel, value, [value, hamiltonian]))
-        acc, hi, lo = call(
-            functools.partial(first_kernel, turns, nrow),
-            blocks[0], hi, lo, [acc_type],
-            [pltpu.VMEM(sig_type.shape, sig_type.dtype)], 2 * flops,
-        )
-        parts0, sig, hi, lo = call(
-            functools.partial(second_kernel, turns, nrow),
-            blocks[1] + [acc], hi, lo, [part, sig_type], [], flops,
-        )
-        parts1, hi, lo = call(
-            functools.partial(third_kernel, turns),
-            [sig, acc], hi, lo, [part], [], flops,
-        )
-        base[0] = small_call(own_kernel, state[0], [base[0], parts0[0]])
-        for a, parts in enumerate((parts0, parts1)):
+        for a in range(CHUNKS):
+            if n > 0:
+                other[a] = partner(state[a])
+            blocks = gather(state[a], other[a])
+            base = small_call(base_kernel, state[a], [state[a], hamiltonian])
+            parts, hi, lo = call(
+                functools.partial(contract_kernel, turns, nrow),
+                blocks, hi, lo, [parts_type],
+                [pltpu.VMEM((2 * total, inner), jnp.bfloat16)],
+                6 * total * inner * outer,
+            )
+            base = small_call(own_kernel, state[a], [base, parts[0]])
             arrived = reduce(parts)
-            total = sum(arrived[2:], arrived[1])
-            if a:
-                total = total + arrived[0]
-            state[a] = base[a] - time_step * total
+            state[a] = base - time_step * sum(arrived[1:], arrived[0])
             rows_out = lax.dynamic_update_slice(
-                rows_out, state[a][None], (n, a * piece, 0, 0)
+                rows_out, state[a][None], (n, 0, a * piece, 0)
             )
     return jnp.transpose(rows_out, (0, 2, 1, 3))
 

time: 129 us -> 132 us (1.023)
  Pallas kernels: 21.3 us -> 26.9 us
  starting transfers between devices: 79.4 us -> 73.9 us
  waiting for transfers between devices: 23.8 us -> 27.7 us
  local copies, waits for them, and re-layouts: 3.68 us -> 2.03 us
    pallas_call x9 -> x6, Pallas kernels: 12.7 us -> 18.3 us  [call(): pl.pallas_call(kernel, in_specs=[pl.BlockSpec(memory_space=VMEM)] * (coun...]
    ppermute x47, starting transfers between devices: 79.4 us -> 73.9 us  [move(): return lax.ppermute(value, AXES, pairs(nrow, ncol, target))]
    ppermute x47, waiting for transfers between devices: 23.8 us -> 27.7 us  [move(): return lax.ppermute(value, AXES, pairs(nrow, ncol, target))]
    unnamed x8 -> x4, local copies, waits for them, and re-layouts: 2.49 us -> 0.82 us
  transfers between devices with their start and end apart: 47 -> 47, of which waited for: 19 -> 16; matrix products, arithmetic and copies ran while one was open for 1% -> 1% of each run, Pallas kernels for 14% -> 21%
where the time goes in v1:
time: 132 us; the launch traced here: 131 us
  starting transfers between devices  73.9 us (56%)
  waiting for transfers between devices  27.7 us (21%)
  Pallas kernels  26.9 us (20%)
  local copies, waits for them, and re-layouts  2.03 us (2%)
    ppermute x47, starting transfers between devices, move(): return lax.ppermute(value, AXES, pairs(nrow, ncol, target))  73.9 us
    ppermute x47, waiting for transfers between devices, move(): return lax.ppermute(value, AXES, pairs(nrow, ncol, target))  27.7 us
    pallas_call x6, Pallas kernels, call(): pl.pallas_call(kernel, in_specs=[pl.BlockSpec(memory_space=VMEM)] * (coun...  18.3 us
    pallas_call x1, Pallas kernels, split_history(): pl.pallas_call(functools.partial(split_kernel, slots), in_specs=[pl.Block...  7.12 us
  transfers between devices with their start and end apart: 47, of which 16 were waited for; matrix products, arithmetic and copies ran while one was open for 1% of the time, Pallas kernels for 21%

profile of v1, /device:TPU:0, one launch (start us, length us, event | category | flops | bytes accessed | tf_op | source)
XLA Modules:
  0.0 131.2 jit_solution(562092579214693523)
XLA Ops:
  0.0 0.5 collective-permute-start
  0.5 1.0 slice_bitcast_fusion.26
  1.8 6.9 %collective-permute-start.1 = (f32[2,12,16,128]{3,2,1,0:T(8,128)S(1)}, f32[2,12,16,128]{3,2,1,0:T(8,128)S(1)}, u32[]{:S(2)}, u32[]{:S(2)}) collective-permute-start(f32[2,12,16,128]{3,2,1,0:T(8,128)S(1)} %pad_maximum_fusion), channel_id=1, source_target_pairs={{0,6},{1,1},{2,14},{3,9},{4,22},{5,17},{6,30},{7,25},{8,4},{9,3},{... | collective-permute-start | bytes 589832 | tf_op jit(solution)/shard_map/ppermute | solution.py:182
  8.7 1.6 %collective-permute-start.2 = (f32[2,12,16,128]{3,2,1,0:T(8,128)S(1)}, f32[2,12,16,128]{3,2,1,0:T(8,128)S(1)}, u32[]{:S(2)}, u32[]{:S(2)}) collective-permute-start(f32[2,12,16,128]{3,2,1,0:T(8,128)S(1)} %pad_maximum_fusion), channel_id=1, source_target_pairs={{0,4},{1,3},{2,12},{3,11},{4,20},{5,19},{6,28},{7,27},{8,6},{9,1},... | collective-permute-start | bytes 589832 | tf_op jit(solution)/shard_map/ppermute | solution.py:182
  10.3 3.2 %collective-permute-start.8 = (f32[2,12,16,128]{3,2,1,0:T(8,128)S(1)}, f32[2,12,16,128]{3,2,1,0:T(8,128)S(1)}, u32[]{:S(2)}, u32[]{:S(2)}) collective-permute-start(f32[2,12,16,128]{3,2,1,0:T(8,128)S(1)} %pad_maximum_fusion.1), channel_id=1, source_target_pairs={{0,6},{1,1},{2,14},{3,9},{4,22},{5,17},{6,30},{7,25},{8,4},{9,3},{... | collective-permute-start | bytes 589832 | tf_op jit(solution)/shard_map/ppermute | solution.py:182
  13.7 2.8 %collective-permute-done.2.refs_1_ = f32[2,12,16,128]{3,2,1,0:T(8,128)S(1)} collective-permute-done((f32[2,12,16,128]{3,2,1,0:T(8,128)S(1)}, f32[2,12,16,128]{3,2,1,0:T(8,128)S(1)}, u32[]{:S(2)}, u32[]{:S(2)}) %collective-permute-start.2) | collective-permute-done | bytes 196640 | tf_op jit(solution)/shard_map/ppermute | solution.py:182
  16.5 7.1 %split_history.1 = (bf16[3072,1536]{1,0:T(8,128)(2,1)S(1)}, bf16[3072,1536]{1,0:T(8,128)(2,1)S(1)}) custom-call(f32[24,12,128,128]{3,2,1,0:T(8,128)} %h_hbm.1), custom_call_target="tpu_custom_call" | custom-call | bytes 37748736 | tf_op jit(solution)/shard_map/split_history/pallas_call | solution.py:53
  24.1 0.6 collective-permute-start.10
  24.8 3.0 %shard_map.38 = (f32[4,12,16,128]{3,2,1,0:T(8,128)S(1)}, bf16[3072,1536]{1,0:T(8,128)(2,1)S(1)}, bf16[3072,1536]{1,0:T(8,128)(2,1)S(1)}) custom-call(f32[2,12,16,128]{3,2,1,0:T(8,128)S(1)} %collective-permute-done.1.refs_0_, f32[2,12,16,128]{3,2,1,0:T(8,128)S(1)} %collective-permute-done.2.refs_1_, ...), custom_call_target="tpu_custom_call", output_to_operand_aliasing={{1}: (4, {}), {2}: (5, {})} | custom-call | flops 1811939328 | bytes 4194304 | tf_op jit(solution)/shard_map/pallas_call | solution.py:128
  27.9 5.3 %collective-permute-start.7 = (f32[12,16,128]{2,1,0:T(8,128)S(1)}, f32[12,16,128]{2,1,0:T(8,128)S(1)}, u32[]{:S(2)}, u32[]{:S(2)}) collective-permute-start(f32[12,16,128]{2,1,0:T(8,128)S(1)} %get-tuple-element.68), channel_id=1, source_target_pairs={{0,24},{1,25},{2,26},{3,27},{4,28},{5,29},{6,30},{7,31},{8,16},{9,... | collective-permute-start | bytes 294920 | tf_op jit(solution)/shard_map/ppermute | solution.py:182
  33.5 0.3 collective-permute-start.6
  33.8 3.0 %shard_map.41 = (f32[4,12,16,128]{3,2,1,0:T(8,128)S(1)}, bf16[3072,1536]{1,0:T(8,128)(2,1)S(1)}, bf16[3072,1536]{1,0:T(8,128)(2,1)S(1)}) custom-call(f32[2,12,16,128]{3,2,1,0:T(8,128)S(1)} %collective-permute-done.8.refs_0_, f32[2,12,16,128]{3,2,1,0:T(8,128)S(1)} %collective-permute-done.9.refs_1_, ...), custom_call_target="tpu_custom_call", output_to_operand_aliasing={{1}: (4, {}), {2}: (5, {})} | custom-call | flops 1811939328 | bytes 4194304 | tf_op jit(solution)/shard_map/pallas_call | solution.py:128
  36.9 2.9 %collective-permute-start.14 = (f32[12,16,128]{2,1,0:T(8,128)S(1)}, f32[12,16,128]{2,1,0:T(8,128)S(1)}, u32[]{:S(2)}, u32[]{:S(2)}) collective-permute-start(f32[12,16,128]{2,1,0:T(8,128)S(1)} %get-tuple-element.64), channel_id=1, source_target_pairs={{0,24},{1,25},{2,26},{3,27},{4,28},{5,29},{6,30},{7,31},{8,16},{9,... | collective-permute-start | bytes 294920 | tf_op jit(solution)/shard_map/ppermute | solution.py:182
  40.2 0.4 collective-permute-start.13
  40.8 2.8 %collective-permute-done.14 = f32[12,16,128]{2,1,0:T(8,128)S(1)} collective-permute-done((f32[12,16,128]{2,1,0:T(8,128)S(1)}, f32[12,16,128]{2,1,0:T(8,128)S(1)}, u32[]{:S(2)}, u32[]{:S(2)}) %collective-permute-start.14) | collective-permute-done | bytes 98336 | tf_op jit(solution)/shard_map/ppermute | solution.py:182
  43.5 1.3 collective-permute-done.12
  45.0 7.8 %collective-permute-start.16 = (f32[2,12,16,128]{3,2,1,0:T(8,128)S(1)}, f32[2,12,16,128]{3,2,1,0:T(8,128)S(1)}, u32[]{:S(2)}, u32[]{:S(2)}) collective-permute-start(f32[2,12,16,128]{3,2,1,0:T(8,128)S(1)} %pad_maximum_fusion.2), channel_id=1, source_target_pairs={{0,6},{1,1},{2,14},{3,9},{4,22},{5,17},{6,30},{7,25},{8,4},{9,3},{... | collective-permute-start | bytes 589832 | tf_op jit(solution)/shard_map/ppermute | solution.py:182
  52.8 1.1 collective-permute-start.17
  54.0 4.0 %collective-permute-start.24 = (f32[2,12,16,128]{3,2,1,0:T(8,128)S(1)}, f32[2,12,16,128]{3,2,1,0:T(8,128)S(1)}, u32[]{:S(2)}, u32[]{:S(2)}) collective-permute-start(f32[2,12,16,128]{3,2,1,0:T(8,128)S(1)} %pad_maximum_fusion.3), channel_id=1, source_target_pairs={{0,6},{1,1},{2,14},{3,9},{4,22},{5,17},{6,30},{7,25},{8,4},{9,3},{... | collective-permute-start | bytes 589832 | tf_op jit(solution)/shard_map/ppermute | solution.py:182
  58.4 1.9 %collective-permute-done.17.refs_1_ = f32[2,12,16,128]{3,2,1,0:T(8,128)S(1)} collective-permute-done((f32[2,12,16,128]{3,2,1,0:T(8,128)S(1)}, f32[2,12,16,128]{3,2,1,0:T(8,128)S(1)}, u32[]{:S(2)}, u32[]{:S(2)}) %collective-permute-start.17) | collective-permute-done | bytes 196640 | tf_op jit(solution)/shard_map/ppermute | solution.py:182
  60.8 2.1 %collective-permute-done.24.refs_0_ = f32[2,12,16,128]{3,2,1,0:T(8,128)S(1)} collective-permute-done((f32[2,12,16,128]{3,2,1,0:T(8,128)S(1)}, f32[2,12,16,128]{3,2,1,0:T(8,128)S(1)}, u32[]{:S(2)}, u32[]{:S(2)}) %collective-permute-start.24) | collective-permute-done | bytes 196640 | tf_op jit(solution)/shard_map/ppermute | solution.py:182
  62.9 2.0 %collective-permute-done.25.refs_1_ = f32[2,12,16,128]{3,2,1,0:T(8,128)S(1)} collective-permute-done((f32[2,12,16,128]{3,2,1,0:T(8,128)S(1)}, f32[2,12,16,128]{3,2,1,0:T(8,128)S(1)}, u32[]{:S(2)}, u32[]{:S(2)}) %collective-permute-start.25) | collective-permute-done | bytes 196640 | tf_op jit(solution)/shard_map/ppermute | solution.py:182
  65.0 3.0 %shard_map.44 = (f32[4,12,16,128]{3,2,1,0:T(8,128)S(1)}, bf16[3072,1536]{1,0:T(8,128)(2,1)S(1)}, bf16[3072,1536]{1,0:T(8,128)(2,1)S(1)}) custom-call(f32[2,12,16,128]{3,2,1,0:T(8,128)S(1)} %collective-permute-done.16.refs_0_, f32[2,12,16,128]{3,2,1,0:T(8,128)S(1)} %collective-permute-done.17.refs_1_, ...), custom_call_target="tpu_custom_call", output_to_operand_aliasing={{1}: (4, {}), {2}: (5, {})} | custom-call | flops 1811939328 | bytes 4194304 | tf_op jit(solution)/shard_map/pallas_call | solution.py:128
  68.0 4.9 %collective-permute-start.22 = (f32[12,16,128]{2,1,0:T(8,128)S(1)}, f32[12,16,128]{2,1,0:T(8,128)S(1)}, u32[]{:S(2)}, u32[]{:S(2)}) collective-permute-start(f32[12,16,128]{2,1,0:T(8,128)S(1)} %get-tuple-element.60), channel_id=1, source_target_pairs={{0,24},{1,25},{2,26},{3,27},{4,28},{5,29},{6,30},{7,31},{8,16},{9,... | collective-permute-start | bytes 294920 | tf_op jit(solution)/shard_map/ppermute | solution.py:182
  73.0 5.4 %collective-permute-start.20 = (f32[12,16,128]{2,1,0:T(8,128)S(1)}, f32[12,16,128]{2,1,0:T(8,128)S(1)}, u32[]{:S(2)}, u32[]{:S(2)}) collective-permute-start(f32[12,16,128]{2,1,0:T(8,128)S(1)} %get-tuple-element.61), channel_id=1, source_target_pairs={{0,8},{1,9},{2,10},{3,11},{4,12},{5,13},{6,14},{7,15},{8,0},{9,1},... | collective-permute-start | bytes 294920 | tf_op jit(solution)/shard_map/ppermute | solution.py:182
  78.3 3.1 %shard_map.47 = (f32[4,12,16,128]{3,2,1,0:T(8,128)S(1)}, bf16[3072,1536]{1,0:T(8,128)(2,1)S(1)}, bf16[3072,1536]{1,0:T(8,128)(2,1)S(1)}) custom-call(f32[2,12,16,128]{3,2,1,0:T(8,128)S(1)} %collective-permute-done.24.refs_0_, f32[2,12,16,128]{3,2,1,0:T(8,128)S(1)} %collective-permute-done.25.refs_1_, ...), custom_call_target="tpu_custom_call", output_to_operand_aliasing={{1}: (4, {}), {2}: (5, {})} | custom-call | flops 1811939328 | bytes 4194304 | tf_op jit(solution)/shard_map/pallas_call | solution.py:128
  81.4 1.5 %collective-permute-start.30 = (f32[12,16,128]{2,1,0:T(8,128)S(1)}, f32[12,16,128]{2,1,0:T(8,128)S(1)}, u32[]{:S(2)}, u32[]{:S(2)}) collective-permute-start(f32[12,16,128]{2,1,0:T(8,128)S(1)} %get-tuple-element.56), channel_id=1, source_target_pairs={{0,24},{1,25},{2,26},{3,27},{4,28},{5,29},{6,30},{7,31},{8,16},{9,... | collective-permute-start | bytes 294920 | tf_op jit(solution)/shard_map/ppermute | solution.py:182
  83.0 2.0 %collective-permute-start.28 = (f32[12,16,128]{2,1,0:T(8,128)S(1)}, f32[12,16,128]{2,1,0:T(8,128)S(1)}, u32[]{:S(2)}, u32[]{:S(2)}) collective-permute-start(f32[12,16,128]{2,1,0:T(8,128)S(1)} %get-tuple-element.57), channel_id=1, source_target_pairs={{0,8},{1,9},{2,10},{3,11},{4,12},{5,13},{6,14},{7,15},{8,0},{9,1},... | collective-permute-start | bytes 294920 | tf_op jit(solution)/shard_map/ppermute | solution.py:182
  85.3 2.4 %collective-permute-done.30 = f32[12,16,128]{2,1,0:T(8,128)S(1)} collective-permute-done((f32[12,16,128]{2,1,0:T(8,128)S(1)}, f32[12,16,128]{2,1,0:T(8,128)S(1)}, u32[]{:S(2)}, u32[]{:S(2)}) %collective-permute-start.30) | collective-permute-done | bytes 98336 | tf_op jit(solution)/shard_map/ppermute | solution.py:182
  87.7 1.2 collective-permute-done.28
  88.9 0.8 collective-permute-done.29
  89.9 4.7 %collective-permute-start.32 = (f32[2,12,16,128]{3,2,1,0:T(8,128)S(1)}, f32[2,12,16,128]{3,2,1,0:T(8,128)S(1)}, u32[]{:S(2)}, u32[]{:S(2)}) collective-permute-start(f32[2,12,16,128]{3,2,1,0:T(8,128)S(1)} %pad_maximum_fusion.4), channel_id=1, source_target_pairs={{0,6},{1,1},{2,14},{3,9},{4,22},{5,17},{6,30},{7,25},{8,4},{9,3},{... | collective-permute-start | bytes 589832 | tf_op jit(solution)/shard_map/ppermute | solution.py:182
  94.6 1.1 collective-permute-start.33
  95.7 3.5 %collective-permute-start.40 = (f32[2,12,16,128]{3,2,1,0:T(8,128)S(1)}, f32[2,12,16,128]{3,2,1,0:T(8,128)S(1)}, u32[]{:S(2)}, u32[]{:S(2)}) collective-permute-start(f32[2,12,16,128]{3,2,1,0:T(8,128)S(1)} %pad_maximum_fusion.5), channel_id=1, source_target_pairs={{0,6},{1,1},{2,14},{3,9},{4,22},{5,17},{6,30},{7,25},{8,4},{9,3},{... | collective-permute-start | bytes 589832 | tf_op jit(solution)/shard_map/ppermute | solution.py:182
  99.2 1.4 %collective-permute-start.41 = (f32[2,12,16,128]{3,2,1,0:T(8,128)S(1)}, f32[2,12,16,128]{3,2,1,0:T(8,128)S(1)}, u32[]{:S(2)}, u32[]{:S(2)}) collective-permute-start(f32[2,12,16,128]{3,2,1,0:T(8,128)S(1)} %pad_maximum_fusion.5), channel_id=1, source_target_pairs={{0,4},{1,3},{2,12},{3,11},{4,20},{5,19},{6,28},{7,27},{8,6},{9,1},... | collective-permute-start | bytes 589832 | tf_op jit(solution)/shard_map/ppermute | solution.py:182
  100.6 1.5 %collective-permute-done.33.refs_1_ = f32[2,12,16,128]{3,2,1,0:T(8,128)S(1)} collective-permute-done((f32[2,12,16,128]{3,2,1,0:T(8,128)S(1)}, f32[2,12,16,128]{3,2,1,0:T(8,128)S(1)}, u32[]{:S(2)}, u32[]{:S(2)}) %collective-permute-start.33) | collective-permute-done | bytes 196640 | tf_op jit(solution)/shard_map/ppermute | solution.py:182
  102.6 1.8 %collective-permute-done.40.refs_0_ = f32[2,12,16,128]{3,2,1,0:T(8,128)S(1)} collective-permute-done((f32[2,12,16,128]{3,2,1,0:T(8,128)S(1)}, f32[2,12,16,128]{3,2,1,0:T(8,128)S(1)}, u32[]{:S(2)}, u32[]{:S(2)}) %collective-permute-start.40) | collective-permute-done | bytes 196640 | tf_op jit(solution)/shard_map/ppermute | solution.py:182
  104.3 2.0 %collective-permute-done.41.refs_1_ = f32[2,12,16,128]{3,2,1,0:T(8,128)S(1)} collective-permute-done((f32[2,12,16,128]{3,2,1,0:T(8,128)S(1)}, f32[2,12,16,128]{3,2,1,0:T(8,128)S(1)}, u32[]{:S(2)}, u32[]{:S(2)}) %collective-permute-start.41) | collective-permute-done | bytes 196640 | tf_op jit(solution)/shard_map/ppermute | solution.py:182
  106.4 3.0 %shard_map.50 = (f32[4,12,16,128]{3,2,1,0:T(8,128)S(1)}, bf16[3072,1536]{1,0:T(8,128)(2,1)S(1)}, bf16[3072,1536]{1,0:T(8,128)(2,1)S(1)}) custom-call(f32[2,12,16,128]{3,2,1,0:T(8,128)S(1)} %collective-permute-done.32.refs_0_, f32[2,12,16,128]{3,2,1,0:T(8,128)S(1)} %collective-permute-done.33.refs_1_, ...), custom_call_target="tpu_custom_call", output_to_operand_aliasing={{1}: (4, {}), {2}: (5, {})} | custom-call | flops 1811939328 | bytes 4194304 | tf_op jit(solution)/shard_map/pallas_call | solution.py:128
  109.4 5.0 %collective-permute-start.38 = (f32[12,16,128]{2,1,0:T(8,128)S(1)}, f32[12,16,128]{2,1,0:T(8,128)S(1)}, u32[]{:S(2)}, u32[]{:S(2)}) collective-permute-start(f32[12,16,128]{2,1,0:T(8,128)S(1)} %get-tuple-element.52), channel_id=1, source_target_pairs={{0,24},{1,25},{2,26},{3,27},{4,28},{5,29},{6,30},{7,31},{8,16},{9,... | collective-permute-start | bytes 294920 | tf_op jit(solution)/shard_map/ppermute | solution.py:182
  114.4 4.6 %collective-permute-start.36 = (f32[12,16,128]{2,1,0:T(8,128)S(1)}, f32[12,16,128]{2,1,0:T(8,128)S(1)}, u32[]{:S(2)}, u32[]{:S(2)}) collective-permute-start(f32[12,16,128]{2,1,0:T(8,128)S(1)} %get-tuple-element.53), channel_id=1, source_target_pairs={{0,8},{1,9},{2,10},{3,11},{4,12},{5,13},{6,14},{7,15},{8,0},{9,1},... | collective-permute-start | bytes 294920 | tf_op jit(solution)/shard_map/ppermute | solution.py:182
  119.0 3.1 %shard_map.53 = (f32[4,12,16,128]{3,2,1,0:T(8,128)S(1)}, bf16[3072,1536]{1,0:T(8,128)(2,1)S(1)}, bf16[3072,1536]{1,0:T(8,128)(2,1)S(1)}) custom-call(f32[2,12,16,128]{3,2,1,0:T(8,128)S(1)} %collective-permute-done.40.refs_0_, f32[2,12,16,128]{3,2,1,0:T(8,128)S(1)} %collective-permute-done.41.refs_1_, ...), custom_call_target="tpu_custom_call", output_to_operand_aliasing={{1}: (4, {}), {2}: (5, {})} | custom-call | flops 1811939328 | bytes 4194304 | tf_op jit(solution)/shard_map/pallas_call | solution.py:128
  122.1 1.5 %collective-permute-start.46 = (f32[12,16,128]{2,1,0:T(8,128)S(1)}, f32[12,16,128]{2,1,0:T(8,128)S(1)}, u32[]{:S(2)}, u32[]{:S(2)}) collective-permute-start(f32[12,16,128]{2,1,0:T(8,128)S(1)} %get-tuple-element.48), channel_id=1, source_target_pairs={{0,24},{1,25},{2,26},{3,27},{4,28},{5,29},{6,30},{7,31},{8,16},{9,... | collective-permute-start | bytes 294920 | tf_op jit(solution)/shard_map/ppermute | solution.py:182
  123.6 2.0 %collective-permute-start.44 = (f32[12,16,128]{2,1,0:T(8,128)S(1)}, f32[12,16,128]{2,1,0:T(8,128)S(1)}, u32[]{:S(2)}, u32[]{:S(2)}) collective-permute-start(f32[12,16,128]{2,1,0:T(8,128)S(1)} %get-tuple-element.49), channel_id=1, source_target_pairs={{0,8},{1,9},{2,10},{3,11},{4,12},{5,13},{6,14},{7,15},{8,0},{9,1},... | collective-permute-start | bytes 294920 | tf_op jit(solution)/shard_map/ppermute | solution.py:182
  125.8 2.5 %collective-permute-done.46 = f32[12,16,128]{2,1,0:T(8,128)S(1)} collective-permute-done((f32[12,16,128]{2,1,0:T(8,128)S(1)}, f32[12,16,128]{2,1,0:T(8,128)S(1)}, u32[]{:S(2)}, u32[]{:S(2)}) %collective-permute-start.46) | collective-permute-done | bytes 98336 | tf_op jit(solution)/shard_map/ppermute | solution.py:182
  128.4 1.2 collective-permute-done.44
  129.6 0.8 collective-permute-done.45
  130.4 0.8 copy-done.1
  (90 shorter events, 4.1 us)
Async XLA Ops:
  0.0 1.8 %collective-permute-start = (f32[12,32,128]{2,1,0:T(8,128)}, f32[12,32,128]{2,1,0:T(8,128)S(1)}, u32[]{:S(2)}, u32[]{:S(2)}) collective-permute-start(f32[12,32,128]{2,1,0:T(8,128)} %bitcast.78), channel_id=1, source_target_pairs={{0,1},{1,0},{2,3},{3,2},{4,5},{5,4},{6,7},{7,6},{8,9},{9,8},{10,11... | collective-permute-start | bytes 589832 | tf_op jit(solution)/shard_map/ppermute | solution.py:182
  1.8 11.9 %collective-permute-start.1 = (f32[2,12,16,128]{3,2,1,0:T(8,128)S(1)}, f32[2,12,16,128]{3,2,1,0:T(8,128)S(1)}, u32[]{:S(2)}, u32[]{:S(2)}) collective-permute-start(f32[2,12,16,128]{3,2,1,0:T(8,128)S(1)} %pad_maximum_fusion), channel_id=1, source_target_pairs={{0,6},{1,1},{2,14},{3,9},{4,22},{5,17},{6,30},{7,25},{8,4},{9,3},{... | collective-permute-start | bytes 589832 | tf_op jit(solution)/shard_map/ppermute | solution.py:182
  8.7 7.8 %collective-permute-start.2 = (f32[2,12,16,128]{3,2,1,0:T(8,128)S(1)}, f32[2,12,16,128]{3,2,1,0:T(8,128)S(1)}, u32[]{:S(2)}, u32[]{:S(2)}) collective-permute-start(f32[2,12,16,128]{3,2,1,0:T(8,128)S(1)} %pad_maximum_fusion), channel_id=1, source_target_pairs={{0,4},{1,3},{2,12},{3,11},{4,20},{5,19},{6,28},{7,27},{8,6},{9,1},... | collective-permute-start | bytes 589832 | tf_op jit(solution)/shard_map/ppermute | solution.py:182
  10.3 13.3 %copy-start = (f32[128,128]{1,0:T(8,128)S(1)}, f32[128,128]{1,0:T(8,128)}, u32[]{:S(2)}) copy-start(f32[128,128]{1,0:T(8,128)} %hamiltonian.11) | copy-start | bytes 196612
  10.3 13.8 %collective-permute-start.8 = (f32[2,12,16,128]{3,2,1,0:T(8,128)S(1)}, f32[2,12,16,128]{3,2,1,0:T(8,128)S(1)}, u32[]{:S(2)}, u32[]{:S(2)}) collective-permute-start(f32[2,12,16,128]{3,2,1,0:T(8,128)S(1)} %pad_maximum_fusion.1), channel_id=1, source_target_pairs={{0,6},{1,1},{2,14},{3,9},{4,22},{5,17},{6,30},{7,25},{8,4},{9,3},{... | collective-permute-start | bytes 589832 | tf_op jit(solution)/shard_map/ppermute | solution.py:182
  13.5 11.3 %collective-permute-start.9 = (f32[2,12,16,128]{3,2,1,0:T(8,128)S(1)}, f32[2,12,16,128]{3,2,1,0:T(8,128)S(1)}, u32[]{:S(2)}, u32[]{:S(2)}) collective-permute-start(f32[2,12,16,128]{3,2,1,0:T(8,128)S(1)} %pad_maximum_fusion.1), channel_id=1, source_target_pairs={{0,4},{1,3},{2,12},{3,11},{4,20},{5,19},{6,28},{7,27},{8,6},{9,1},... | collective-permute-start | bytes 589832 | tf_op jit(solution)/shard_map/ppermute | solution.py:182
  13.7 11.1 %collective-permute-start.3 = (f32[2,12,16,128]{3,2,1,0:T(8,128)S(1)}, f32[2,12,16,128]{3,2,1,0:T(8,128)S(1)}, u32[]{:S(2)}, u32[]{:S(2)}) collective-permute-start(f32[2,12,16,128]{3,2,1,0:T(8,128)S(1)} %collective-permute-done.1.refs_0_), channel_id=1, source_target_pairs={{0,1},{1,0},{2,3},{3,2},{4,5},{5,4},{6,7},{7,6},{8,9},{9,8},{10,11... | collective-permute-start | bytes 589832 | tf_op jit(solution)/shard_map/ppermute | solution.py:182
  16.5 8.3 %collective-permute-start.4 = (f32[2,12,16,128]{3,2,1,0:T(8,128)S(1)}, f32[2,12,16,128]{3,2,1,0:T(8,128)S(1)}, u32[]{:S(2)}, u32[]{:S(2)}) collective-permute-start(f32[2,12,16,128]{3,2,1,0:T(8,128)S(1)} %collective-permute-done.2.refs_1_), channel_id=1, source_target_pairs={{0,1},{1,0},{2,3},{3,2},{4,5},{5,4},{6,7},{7,6},{8,9},{9,8},{10,11... | collective-permute-start | bytes 589832 | tf_op jit(solution)/shard_map/ppermute | solution.py:182
  24.1 9.7 %collective-permute-start.10 = (f32[2,12,16,128]{3,2,1,0:T(8,128)S(1)}, f32[2,12,16,128]{3,2,1,0:T(8,128)S(1)}, u32[]{:S(2)}, u32[]{:S(2)}) collective-permute-start(f32[2,12,16,128]{3,2,1,0:T(8,128)S(1)} %collective-permute-done.8.refs_0_), channel_id=1, source_target_pairs={{0,1},{1,0},{2,3},{3,2},{4,5},{5,4},{6,7},{7,6},{8,9},{9,8},{10,11... | collective-permute-start | bytes 589832 | tf_op jit(solution)/shard_map/ppermute | solution.py:182
  24.7 9.1 %collective-permute-start.11 = (f32[2,12,16,128]{3,2,1,0:T(8,128)S(1)}, f32[2,12,16,128]{3,2,1,0:T(8,128)S(1)}, u32[]{:S(2)}, u32[]{:S(2)}) collective-permute-start(f32[2,12,16,128]{3,2,1,0:T(8,128)S(1)} %collective-permute-done.9.refs_1_), channel_id=1, source_target_pairs={{0,1},{1,0},{2,3},{3,2},{4,5},{5,4},{6,7},{7,6},{8,9},{9,8},{10,11... | collective-permute-start | bytes 589832 | tf_op jit(solution)/shard_map/ppermute | solution.py:182
  27.9 12.3 %collective-permute-start.7 = (f32[12,16,128]{2,1,0:T(8,128)S(1)}, f32[12,16,128]{2,1,0:T(8,128)S(1)}, u32[]{:S(2)}, u32[]{:S(2)}) collective-permute-start(f32[12,16,128]{2,1,0:T(8,128)S(1)} %get-tuple-element.68), channel_id=1, source_target_pairs={{0,24},{1,25},{2,26},{3,27},{4,28},{5,29},{6,30},{7,31},{8,16},{9,... | collective-permute-start | bytes 294920 | tf_op jit(solution)/shard_map/ppermute | solution.py:182
  33.2 7.4 %collective-permute-start.5 = (f32[12,16,128]{2,1,0:T(8,128)S(1)}, f32[12,16,128]{2,1,0:T(8,128)S(1)}, u32[]{:S(2)}, u32[]{:S(2)}) collective-permute-start(f32[12,16,128]{2,1,0:T(8,128)S(1)} %get-tuple-element.69), channel_id=1, source_target_pairs={{0,8},{1,9},{2,10},{3,11},{4,12},{5,13},{6,14},{7,15},{8,0},{9,1},... | collective-permute-start | bytes 294920 | tf_op jit(solution)/shard_map/ppermute | solution.py:182
  33.5 7.1 %collective-permute-start.6 = (f32[12,16,128]{2,1,0:T(8,128)S(1)}, f32[12,16,128]{2,1,0:T(8,128)S(1)}, u32[]{:S(2)}, u32[]{:S(2)}) collective-permute-start(f32[12,16,128]{2,1,0:T(8,128)S(1)} %get-tuple-element.67), channel_id=1, source_target_pairs={{0,16},{1,17},{2,18},{3,19},{4,20},{5,21},{6,22},{7,23},{8,24},{9,... | collective-permute-start | bytes 294920 | tf_op jit(solution)/shard_map/ppermute | solution.py:182
  36.9 6.6 %collective-permute-start.14 = (f32[12,16,128]{2,1,0:T(8,128)S(1)}, f32[12,16,128]{2,1,0:T(8,128)S(1)}, u32[]{:S(2)}, u32[]{:S(2)}) collective-permute-start(f32[12,16,128]{2,1,0:T(8,128)S(1)} %get-tuple-element.64), channel_id=1, source_target_pairs={{0,24},{1,25},{2,26},{3,27},{4,28},{5,29},{6,30},{7,31},{8,16},{9,... | collective-permute-start | bytes 294920 | tf_op jit(solution)/shard_map/ppermute | solution.py:182
  39.8 5.0 %collective-permute-start.12 = (f32[12,16,128]{2,1,0:T(8,128)S(1)}, f32[12,16,128]{2,1,0:T(8,128)S(1)}, u32[]{:S(2)}, u32[]{:S(2)}) collective-permute-start(f32[12,16,128]{2,1,0:T(8,128)S(1)} %get-tuple-element.65), channel_id=1, source_target_pairs={{0,8},{1,9},{2,10},{3,11},{4,12},{5,13},{6,14},{7,15},{8,0},{9,1},... | collective-permute-start | bytes 294920 | tf_op jit(solution)/shard_map/ppermute | solution.py:182
  40.2 4.7 %collective-permute-start.13 = (f32[12,16,128]{2,1,0:T(8,128)S(1)}, f32[12,16,128]{2,1,0:T(8,128)S(1)}, u32[]{:S(2)}, u32[]{:S(2)}) collective-permute-start(f32[12,16,128]{2,1,0:T(8,128)S(1)} %get-tuple-element.63), channel_id=1, source_target_pairs={{0,16},{1,17},{2,18},{3,19},{4,20},{5,21},{6,22},{7,23},{8,24},{9,... | collective-permute-start | bytes 294920 | tf_op jit(solution)/shard_map/ppermute | solution.py:182
  40.6 4.4 %collective-permute-start.15 = (f32[12,16,128]{2,1,0:T(8,128)S(1)}, f32[12,16,128]{2,1,0:T(8,128)S(1)}, u32[]{:S(2)}, u32[]{:S(2)}) collective-permute-start(f32[12,16,128]{2,1,0:T(8,128)S(1)} %multiply_subtract_fusion.3.value), channel_id=1, source_target_pairs={{0,1},{1,0},{2,3},{3,2},{4,5},{5,4},{6,7},{7,6},{8,9},{9,8},{10,11... | collective-permute-start | bytes 294920 | tf_op jit(solution)/shard_map/ppermute | solution.py:182
  44.9 9.1 %collective-permute-start.23 = (f32[12,16,128]{2,1,0:T(8,128)S(1)}, f32[12,16,128]{2,1,0:T(8,128)S(1)}, u32[]{:S(2)}, u32[]{:S(2)}) collective-permute-start(f32[12,16,128]{2,1,0:T(8,128)S(1)} %get-tuple-element.46.value), channel_id=1, source_target_pairs={{0,1},{1,0},{2,3},{3,2},{4,5},{5,4},{6,7},{7,6},{8,9},{9,8},{10,11... | collective-permute-start | bytes 294920 | tf_op jit(solution)/shard_map/ppermute | solution.py:182
  45.0 13.3 %collective-permute-start.16 = (f32[2,12,16,128]{3,2,1,0:T(8,128)S(1)}, f32[2,12,16,128]{3,2,1,0:T(8,128)S(1)}, u32[]{:S(2)}, u32[]{:S(2)}) collective-permute-start(f32[2,12,16,128]{3,2,1,0:T(8,128)S(1)} %pad_maximum_fusion.2), channel_id=1, source_target_pairs={{0,6},{1,1},{2,14},{3,9},{4,22},{5,17},{6,30},{7,25},{8,4},{9,3},{... | collective-permute-start | bytes 589832 | tf_op jit(solution)/shard_map/ppermute | solution.py:182
  52.8 7.5 %collective-permute-start.17 = (f32[2,12,16,128]{3,2,1,0:T(8,128)S(1)}, f32[2,12,16,128]{3,2,1,0:T(8,128)S(1)}, u32[]{:S(2)}, u32[]{:S(2)}) collective-permute-start(f32[2,12,16,128]{3,2,1,0:T(8,128)S(1)} %pad_maximum_fusion.2), channel_id=1, source_target_pairs={{0,4},{1,3},{2,12},{3,11},{4,20},{5,19},{6,28},{7,27},{8,6},{9,1},... | collective-permute-start | bytes 589832 | tf_op jit(solution)/shard_map/ppermute | solution.py:182
  54.0 9.0 %collective-permute-start.24 = (f32[2,12,16,128]{3,2,1,0:T(8,128)S(1)}, f32[2,12,16,128]{3,2,1,0:T(8,128)S(1)}, u32[]{:S(2)}, u32[]{:S(2)}) collective-permute-start(f32[2,12,16,128]{3,2,1,0:T(8,128)S(1)} %pad_maximum_fusion.3), channel_id=1, source_target_pairs={{0,6},{1,1},{2,14},{3,9},{4,22},{5,17},{6,30},{7,25},{8,4},{9,3},{... | collective-permute-start | bytes 589832 | tf_op jit(solution)/shard_map/ppermute | solution.py:182
  58.0 6.9 %collective-permute-start.25 = (f32[2,12,16,128]{3,2,1,0:T(8,128)S(1)}, f32[2,12,16,128]{3,2,1,0:T(8,128)S(1)}, u32[]{:S(2)}, u32[]{:S(2)}) collective-permute-start(f32[2,12,16,128]{3,2,1,0:T(8,128)S(1)} %pad_maximum_fusion.3), channel_id=1, source_target_pairs={{0,4},{1,3},{2,12},{3,11},{4,20},{5,19},{6,28},{7,27},{8,6},{9,1},... | collective-permute-start | bytes 589832 | tf_op jit(solution)/shard_map/ppermute | solution.py:182
  58.3 6.7 %collective-permute-start.18 = (f32[2,12,16,128]{3,2,1,0:T(8,128)S(1)}, f32[2,12,16,128]{3,2,1,0:T(8,128)S(1)}, u32[]{:S(2)}, u32[]{:S(2)}) collective-permute-start(f32[2,12,16,128]{3,2,1,0:T(8,128)S(1)} %collective-permute-done.16.refs_0_), channel_id=1, source_target_pairs={{0,1},{1,0},{2,3},{3,2},{4,5},{5,4},{6,7},{7,6},{8,9},{9,8},{10,11... | collective-permute-start | bytes 589832 | tf_op jit(solution)/shard_map/ppermute | solution.py:182
  60.3 4.7 %collective-permute-start.19 = (f32[2,12,16,128]{3,2,1,0:T(8,128)S(1)}, f32[2,12,16,128]{3,2,1,0:T(8,128)S(1)}, u32[]{:S(2)}, u32[]{:S(2)}) collective-permute-start(f32[2,12,16,128]{3,2,1,0:T(8,128)S(1)} %collective-permute-done.17.refs_1_), channel_id=1, source_target_pairs={{0,1},{1,0},{2,3},{3,2},{4,5},{5,4},{6,7},{7,6},{8,9},{9,8},{10,11... | collective-permute-start | bytes 589832 | tf_op jit(solution)/shard_map/ppermute | solution.py:182
  62.9 15.4 %collective-permute-start.26 = (f32[2,12,16,128]{3,2,1,0:T(8,128)S(1)}, f32[2,12,16,128]{3,2,1,0:T(8,128)S(1)}, u32[]{:S(2)}, u32[]{:S(2)}) collective-permute-start(f32[2,12,16,128]{3,2,1,0:T(8,128)S(1)} %collective-permute-done.24.refs_0_), channel_id=1, source_target_pairs={{0,1},{1,0},{2,3},{3,2},{4,5},{5,4},{6,7},{7,6},{8,9},{9,8},{10,11... | collective-permute-start | bytes 589832 | tf_op jit(solution)/shard_map/ppermute | solution.py:182
  65.0 13.4 %collective-permute-start.27 = (f32[2,12,16,128]{3,2,1,0:T(8,128)S(1)}, f32[2,12,16,128]{3,2,1,0:T(8,128)S(1)}, u32[]{:S(2)}, u32[]{:S(2)}) collective-permute-start(f32[2,12,16,128]{3,2,1,0:T(8,128)S(1)} %collective-permute-done.25.refs_1_), channel_id=1, source_target_pairs={{0,1},{1,0},{2,3},{3,2},{4,5},{5,4},{6,7},{7,6},{8,9},{9,8},{10,11... | collective-permute-start | bytes 589832 | tf_op jit(solution)/shard_map/ppermute | solution.py:182
  68.0 17.0 %collective-permute-start.22 = (f32[12,16,128]{2,1,0:T(8,128)S(1)}, f32[12,16,128]{2,1,0:T(8,128)S(1)}, u32[]{:S(2)}, u32[]{:S(2)}) collective-permute-start(f32[12,16,128]{2,1,0:T(8,128)S(1)} %get-tuple-element.60), channel_id=1, source_target_pairs={{0,24},{1,25},{2,26},{3,27},{4,28},{5,29},{6,30},{7,31},{8,16},{9,... | collective-permute-start | bytes 294920 | tf_op jit(solution)/shard_map/ppermute | solution.py:182
  73.0 12.1 %collective-permute-start.20 = (f32[12,16,128]{2,1,0:T(8,128)S(1)}, f32[12,16,128]{2,1,0:T(8,128)S(1)}, u32[]{:S(2)}, u32[]{:S(2)}) collective-permute-start(f32[12,16,128]{2,1,0:T(8,128)S(1)} %get-tuple-element.61), channel_id=1, source_target_pairs={{0,8},{1,9},{2,10},{3,11},{4,12},{5,13},{6,14},{7,15},{8,0},{9,1},... | collective-permute-start | bytes 294920 | tf_op jit(solution)/shard_map/ppermute | solution.py:182
  78.3 6.8 %collective-permute-start.21 = (f32[12,16,128]{2,1,0:T(8,128)S(1)}, f32[12,16,128]{2,1,0:T(8,128)S(1)}, u32[]{:S(2)}, u32[]{:S(2)}) collective-permute-start(f32[12,16,128]{2,1,0:T(8,128)S(1)} %get-tuple-element.59), channel_id=1, source_target_pairs={{0,16},{1,17},{2,18},{3,19},{4,20},{5,21},{6,22},{7,23},{8,24},{9,... | collective-permute-start | bytes 294920 | tf_op jit(solution)/shard_map/ppermute | solution.py:182
  81.4 6.3 %collective-permute-start.30 = (f32[12,16,128]{2,1,0:T(8,128)S(1)}, f32[12,16,128]{2,1,0:T(8,128)S(1)}, u32[]{:S(2)}, u32[]{:S(2)}) collective-permute-start(f32[12,16,128]{2,1,0:T(8,128)S(1)} %get-tuple-element.56), channel_id=1, source_target_pairs={{0,24},{1,25},{2,26},{3,27},{4,28},{5,29},{6,30},{7,31},{8,16},{9,... | collective-permute-start | bytes 294920 | tf_op jit(solution)/shard_map/ppermute | solution.py:182
  83.0 6.0 %collective-permute-start.28 = (f32[12,16,128]{2,1,0:T(8,128)S(1)}, f32[12,16,128]{2,1,0:T(8,128)S(1)}, u32[]{:S(2)}, u32[]{:S(2)}) collective-permute-start(f32[12,16,128]{2,1,0:T(8,128)S(1)} %get-tuple-element.57), channel_id=1, source_target_pairs={{0,8},{1,9},{2,10},{3,11},{4,12},{5,13},{6,14},{7,15},{8,0},{9,1},... | collective-permute-start | bytes 294920 | tf_op jit(solution)/shard_map/ppermute | solution.py:182
  85.0 4.7 %collective-permute-start.29 = (f32[12,16,128]{2,1,0:T(8,128)S(1)}, f32[12,16,128]{2,1,0:T(8,128)S(1)}, u32[]{:S(2)}, u32[]{:S(2)}) collective-permute-start(f32[12,16,128]{2,1,0:T(8,128)S(1)} %get-tuple-element.55), channel_id=1, source_target_pairs={{0,16},{1,17},{2,18},{3,19},{4,20},{5,21},{6,22},{7,23},{8,24},{9,... | collective-permute-start | bytes 294920 | tf_op jit(solution)/shard_map/ppermute | solution.py:182
  85.2 4.7 %collective-permute-start.31 = (f32[12,16,128]{2,1,0:T(8,128)S(1)}, f32[12,16,128]{2,1,0:T(8,128)S(1)}, u32[]{:S(2)}, u32[]{:S(2)}) collective-permute-start(f32[12,16,128]{2,1,0:T(8,128)S(1)} %get-tuple-element.44.value), channel_id=1, source_target_pairs={{0,1},{1,0},{2,3},{3,2},{4,5},{5,4},{6,7},{7,6},{8,9},{9,8},{10,11... | collective-permute-start | bytes 294920 | tf_op jit(solution)/shard_map/ppermute | solution.py:182
  89.7 5.9 %collective-permute-start.39 = (f32[12,16,128]{2,1,0:T(8,128)S(1)}, f32[12,16,128]{2,1,0:T(8,128)S(1)}, u32[]{:S(2)}, u32[]{:S(2)}) collective-permute-start(f32[12,16,128]{2,1,0:T(8,128)S(1)} %get-tuple-element.42.value), channel_id=1, source_target_pairs={{0,1},{1,0},{2,3},{3,2},{4,5},{5,4},{6,7},{7,6},{8,9},{9,8},{10,11... | collective-permute-start | bytes 294920 | tf_op jit(solution)/shard_map/ppermute | solution.py:182
  89.9 10.7 %collective-permute-start.32 = (f32[2,12,16,128]{3,2,1,0:T(8,128)S(1)}, f32[2,12,16,128]{3,2,1,0:T(8,128)S(1)}, u32[]{:S(2)}, u32[]{:S(2)}) collective-permute-start(f32[2,12,16,128]{3,2,1,0:T(8,128)S(1)} %pad_maximum_fusion.4), channel_id=1, source_target_pairs={{0,6},{1,1},{2,14},{3,9},{4,22},{5,17},{6,30},{7,25},{8,4},{9,3},{... | collective-permute-start | bytes 589832 | tf_op jit(solution)/shard_map/ppermute | solution.py:182
  94.6 7.5 %collective-permute-start.33 = (f32[2,12,16,128]{3,2,1,0:T(8,128)S(1)}, f32[2,12,16,128]{3,2,1,0:T(8,128)S(1)}, u32[]{:S(2)}, u32[]{:S(2)}) collective-permute-start(f32[2,12,16,128]{3,2,1,0:T(8,128)S(1)} %pad_maximum_fusion.4), channel_id=1, source_target_pairs={{0,4},{1,3},{2,12},{3,11},{4,20},{5,19},{6,28},{7,27},{8,6},{9,1},... | collective-permute-start | bytes 589832 | tf_op jit(solution)/shard_map/ppermute | solution.py:182
  95.7 8.7 %collective-permute-start.40 = (f32[2,12,16,128]{3,2,1,0:T(8,128)S(1)}, f32[2,12,16,128]{3,2,1,0:T(8,128)S(1)}, u32[]{:S(2)}, u32[]{:S(2)}) collective-permute-start(f32[2,12,16,128]{3,2,1,0:T(8,128)S(1)} %pad_maximum_fusion.5), channel_id=1, source_target_pairs={{0,6},{1,1},{2,14},{3,9},{4,22},{5,17},{6,30},{7,25},{8,4},{9,3},{... | collective-permute-start | bytes 589832 | tf_op jit(solution)/shard_map/ppermute | solution.py:182
  99.2 7.2 %collective-permute-start.41 = (f32[2,12,16,128]{3,2,1,0:T(8,128)S(1)}, f32[2,12,16,128]{3,2,1,0:T(8,128)S(1)}, u32[]{:S(2)}, u32[]{:S(2)}) collective-permute-start(f32[2,12,16,128]{3,2,1,0:T(8,128)S(1)} %pad_maximum_fusion.5), channel_id=1, source_target_pairs={{0,4},{1,3},{2,12},{3,11},{4,20},{5,19},{6,28},{7,27},{8,6},{9,1},... | collective-permute-start | bytes 589832 | tf_op jit(solution)/shard_map/ppermute | solution.py:182
  100.6 5.8 %collective-permute-start.34 = (f32[2,12,16,128]{3,2,1,0:T(8,128)S(1)}, f32[2,12,16,128]{3,2,1,0:T(8,128)S(1)}, u32[]{:S(2)}, u32[]{:S(2)}) collective-permute-start(f32[2,12,16,128]{3,2,1,0:T(8,128)S(1)} %collective-permute-done.32.refs_0_), channel_id=1, source_target_pairs={{0,1},{1,0},{2,3},{3,2},{4,5},{5,4},{6,7},{7,6},{8,9},{9,8},{10,11... | collective-permute-start | bytes 589832 | tf_op jit(solution)/shard_map/ppermute | solution.py:182
  102.1 4.3 %collective-permute-start.35 = (f32[2,12,16,128]{3,2,1,0:T(8,128)S(1)}, f32[2,12,16,128]{3,2,1,0:T(8,128)S(1)}, u32[]{:S(2)}, u32[]{:S(2)}) collective-permute-start(f32[2,12,16,128]{3,2,1,0:T(8,128)S(1)} %collective-permute-done.33.refs_1_), channel_id=1, source_target_pairs={{0,1},{1,0},{2,3},{3,2},{4,5},{5,4},{6,7},{7,6},{8,9},{9,8},{10,11... | collective-permute-start | bytes 589832 | tf_op jit(solution)/shard_map/ppermute | solution.py:182
  104.3 14.7 %collective-permute-start.42 = (f32[2,12,16,128]{3,2,1,0:T(8,128)S(1)}, f32[2,12,16,128]{3,2,1,0:T(8,128)S(1)}, u32[]{:S(2)}, u32[]{:S(2)}) collective-permute-start(f32[2,12,16,128]{3,2,1,0:T(8,128)S(1)} %collective-permute-done.40.refs_0_), channel_id=1, source_target_pairs={{0,1},{1,0},{2,3},{3,2},{4,5},{5,4},{6,7},{7,6},{8,9},{9,8},{10,11... | collective-permute-start | bytes 589832 | tf_op jit(solution)/shard_map/ppermute | solution.py:182
  106.3 12.7 %collective-permute-start.43 = (f32[2,12,16,128]{3,2,1,0:T(8,128)S(1)}, f32[2,12,16,128]{3,2,1,0:T(8,128)S(1)}, u32[]{:S(2)}, u32[]{:S(2)}) collective-permute-start(f32[2,12,16,128]{3,2,1,0:T(8,128)S(1)} %collective-permute-done.41.refs_1_), channel_id=1, source_target_pairs={{0,1},{1,0},{2,3},{3,2},{4,5},{5,4},{6,7},{7,6},{8,9},{9,8},{10,11... | collective-permute-start | bytes 589832 | tf_op jit(solution)/shard_map/ppermute | solution.py:182
  109.4 16.2 %collective-permute-start.38 = (f32[12,16,128]{2,1,0:T(8,128)S(1)}, f32[12,16,128]{2,1,0:T(8,128)S(1)}, u32[]{:S(2)}, u32[]{:S(2)}) collective-permute-start(f32[12,16,128]{2,1,0:T(8,128)S(1)} %get-tuple-element.52), channel_id=1, source_target_pairs={{0,24},{1,25},{2,26},{3,27},{4,28},{5,29},{6,30},{7,31},{8,16},{9,... | collective-permute-start | bytes 294920 | tf_op jit(solution)/shard_map/ppermute | solution.py:182
  114.4 11.3 %collective-permute-start.36 = (f32[12,16,128]{2,1,0:T(8,128)S(1)}, f32[12,16,128]{2,1,0:T(8,128)S(1)}, u32[]{:S(2)}, u32[]{:S(2)}) collective-permute-start(f32[12,16,128]{2,1,0:T(8,128)S(1)} %get-tuple-element.53), channel_id=1, source_target_pairs={{0,8},{1,9},{2,10},{3,11},{4,12},{5,13},{6,14},{7,15},{8,0},{9,1},... | collective-permute-start | bytes 294920 | tf_op jit(solution)/shard_map/ppermute | solution.py:182
  119.0 6.8 %collective-permute-start.37 = (f32[12,16,128]{2,1,0:T(8,128)S(1)}, f32[12,16,128]{2,1,0:T(8,128)S(1)}, u32[]{:S(2)}, u32[]{:S(2)}) collective-permute-start(f32[12,16,128]{2,1,0:T(8,128)S(1)} %get-tuple-element.51), channel_id=1, source_target_pairs={{0,16},{1,17},{2,18},{3,19},{4,20},{5,21},{6,22},{7,23},{8,24},{9,... | collective-permute-start | bytes 294920 | tf_op jit(solution)/shard_map/ppermute | solution.py:182
  122.1 6.3 %collective-permute-start.46 = (f32[12,16,128]{2,1,0:T(8,128)S(1)}, f32[12,16,128]{2,1,0:T(8,128)S(1)}, u32[]{:S(2)}, u32[]{:S(2)}) collective-permute-start(f32[12,16,128]{2,1,0:T(8,128)S(1)} %get-tuple-element.48), channel_id=1, source_target_pairs={{0,24},{1,25},{2,26},{3,27},{4,28},{5,29},{6,30},{7,31},{8,16},{9,... | collective-permute-start | bytes 294920 | tf_op jit(solution)/shard_map/ppermute | solution.py:182
  123.6 6.0 %collective-permute-start.44 = (f32[12,16,128]{2,1,0:T(8,128)S(1)}, f32[12,16,128]{2,1,0:T(8,128)S(1)}, u32[]{:S(2)}, u32[]{:S(2)}) collective-permute-start(f32[12,16,128]{2,1,0:T(8,128)S(1)} %get-tuple-element.49), channel_id=1, source_target_pairs={{0,8},{1,9},{2,10},{3,11},{4,12},{5,13},{6,14},{7,15},{8,0},{9,1},... | collective-permute-start | bytes 294920 | tf_op jit(solution)/shard_map/ppermute | solution.py:182
  125.7 4.7 %collective-permute-start.45 = (f32[12,16,128]{2,1,0:T(8,128)S(1)}, f32[12,16,128]{2,1,0:T(8,128)S(1)}, u32[]{:S(2)}, u32[]{:S(2)}) collective-permute-start(f32[12,16,128]{2,1,0:T(8,128)S(1)} %get-tuple-element.47), channel_id=1, source_target_pairs={{0,16},{1,17},{2,18},{3,19},{4,20},{5,21},{6,22},{7,23},{8,24},{9,... | collective-permute-start | bytes 294920 | tf_op jit(solution)/shard_map/ppermute | solution.py:182
  (1 other events, 0.8 us)

commit v2 on v1

--- a/solution.py
+++ b/solution.py
@@ -13,6 +13,8 @@
 CHUNKS = 2
 
 time_step = 0.2
+
+LARGEST = float(jnp.finfo(jnp.bfloat16).max)
 
 AXES = ("row", "col")
 VMEM = pltpu.VMEM
@@ -88,7 +90,7 @@
             for t in range(cols):
                 x = blocks[b][first ^ half, t]
                 x = x * x * x
-                high = x.astype(jnp.bfloat16)
+                high = jnp.clip(x, -LARGEST, LARGEST).astype(jnp.bfloat16)
                 s = half * cols + t
                 at = slice(s * depth, (s + 1) * depth)
                 sig[b * rows : (b + 1) * rows, at] = high
@@ -113,7 +115,7 @@
     fill(turns, blocks, sig)
     total = sig.shape[0] // 2
     cols, _, width = out.shape[1:]
-    group = 4 if cols % 4 == 0 else 1
+    group = cols
     for t0 in range(0, cols, group):
         at = slice(t0 * width, (t0 + group) * width)
         both = jnp.dot(sig[...], hi[:, at], preferred_element_type=jnp.float32)

time: 132 us -> 131 us (level)
  transfers between devices with their start and end apart: 47 -> 47, of which waited for: 16 -> 16; matrix products, arithmetic and copies ran while one was open for 1% -> 1% of each run, Pallas kernels for 21% -> 20%
where the time goes in v2:
time: 131 us
  starting transfers between devices  73.9 us (56%)
  waiting for transfers between devices  27.7 us (21%)
  Pallas kernels  26.7 us (20%)
  local copies, waits for them, and re-layouts  2.03 us (2%)
    ppermute x47, starting transfers between devices, move(): return lax.ppermute(value, AXES, pairs(nrow, ncol, target))  73.9 us
    ppermute x47, waiting for transfers between devices, move(): return lax.ppermute(value, AXES, pairs(nrow, ncol, target))  27.7 us
    pallas_call x6, Pallas kernels, call(): pl.pallas_call(kernel, in_specs=[pl.BlockSpec(memory_space=VMEM)] * (coun...  18 us
    pallas_call x1, Pallas kernels, split_history(): pl.pallas_call(functools.partial(split_kernel, slots), in_specs=[pl.Block...  7.12 us
  transfers between devices with their start and end apart: 47, of which 16 were waited for; matrix products, arithmetic and copies ran while one was open for 1% of the time, Pallas kernels for 20%

profile of v2, /device:TPU:0, one launch (start us, length us, event | category | flops | bytes accessed | tf_op | source)
XLA Modules:
  0.0 131.0 jit_solution(16491785029308372945)
XLA Ops:
  0.0 0.5 collective-permute-start
  0.5 1.0 slice_bitcast_fusion.26
  1.8 6.9 %collective-permute-start.1 = (f32[2,12,16,128]{3,2,1,0:T(8,128)S(1)}, f32[2,12,16,128]{3,2,1,0:T(8,128)S(1)}, u32[]{:S(2)}, u32[]{:S(2)}) collective-permute-start(f32[2,12,16,128]{3,2,1,0:T(8,128)S(1)} %pad_maximum_fusion), channel_id=1, source_target_pairs={{0,6},{1,1},{2,14},{3,9},{4,22},{5,17},{6,30},{7,25},{8,4},{9,3},{... | collective-permute-start | bytes 589832 | tf_op jit(solution)/shard_map/ppermute | solution.py:184
  8.7 1.6 %collective-permute-start.2 = (f32[2,12,16,128]{3,2,1,0:T(8,128)S(1)}, f32[2,12,16,128]{3,2,1,0:T(8,128)S(1)}, u32[]{:S(2)}, u32[]{:S(2)}) collective-permute-start(f32[2,12,16,128]{3,2,1,0:T(8,128)S(1)} %pad_maximum_fusion), channel_id=1, source_target_pairs={{0,4},{1,3},{2,12},{3,11},{4,20},{5,19},{6,28},{7,27},{8,6},{9,1},... | collective-permute-start | bytes 589832 | tf_op jit(solution)/shard_map/ppermute | solution.py:184
  10.3 3.2 %collective-permute-start.8 = (f32[2,12,16,128]{3,2,1,0:T(8,128)S(1)}, f32[2,12,16,128]{3,2,1,0:T(8,128)S(1)}, u32[]{:S(2)}, u32[]{:S(2)}) collective-permute-start(f32[2,12,16,128]{3,2,1,0:T(8,128)S(1)} %pad_maximum_fusion.1), channel_id=1, source_target_pairs={{0,6},{1,1},{2,14},{3,9},{4,22},{5,17},{6,30},{7,25},{8,4},{9,3},{... | collective-permute-start | bytes 589832 | tf_op jit(solution)/shard_map/ppermute | solution.py:184
  13.7 2.8 %collective-permute-done.2.refs_1_ = f32[2,12,16,128]{3,2,1,0:T(8,128)S(1)} collective-permute-done((f32[2,12,16,128]{3,2,1,0:T(8,128)S(1)}, f32[2,12,16,128]{3,2,1,0:T(8,128)S(1)}, u32[]{:S(2)}, u32[]{:S(2)}) %collective-permute-start.2) | collective-permute-done | bytes 196640 | tf_op jit(solution)/shard_map/ppermute | solution.py:184
  16.5 7.1 %split_history.1 = (bf16[3072,1536]{1,0:T(8,128)(2,1)S(1)}, bf16[3072,1536]{1,0:T(8,128)(2,1)S(1)}) custom-call(f32[24,12,128,128]{3,2,1,0:T(8,128)} %h_hbm.1), custom_call_target="tpu_custom_call" | custom-call | bytes 37748736 | tf_op jit(solution)/shard_map/split_history/pallas_call | solution.py:55
  24.1 0.6 collective-permute-start.10
  24.8 3.0 %shard_map.38 = (f32[4,12,16,128]{3,2,1,0:T(8,128)S(1)}, bf16[3072,1536]{1,0:T(8,128)(2,1)S(1)}, bf16[3072,1536]{1,0:T(8,128)(2,1)S(1)}) custom-call(f32[2,12,16,128]{3,2,1,0:T(8,128)S(1)} %collective-permute-done.1.refs_0_, f32[2,12,16,128]{3,2,1,0:T(8,128)S(1)} %collective-permute-done.2.refs_1_, ...), custom_call_target="tpu_custom_call", output_to_operand_aliasing={{1}: (4, {}), {2}: (5, {})} | custom-call | flops 1811939328 | bytes 4194304 | tf_op jit(solution)/shard_map/pallas_call | solution.py:130
  27.8 5.3 %collective-permute-start.7 = (f32[12,16,128]{2,1,0:T(8,128)S(1)}, f32[12,16,128]{2,1,0:T(8,128)S(1)}, u32[]{:S(2)}, u32[]{:S(2)}) collective-permute-start(f32[12,16,128]{2,1,0:T(8,128)S(1)} %get-tuple-element.68), channel_id=1, source_target_pairs={{0,24},{1,25},{2,26},{3,27},{4,28},{5,29},{6,30},{7,31},{8,16},{9,... | collective-permute-start | bytes 294920 | tf_op jit(solution)/shard_map/ppermute | solution.py:184
  33.4 0.3 collective-permute-start.6
  33.8 3.0 %shard_map.41 = (f32[4,12,16,128]{3,2,1,0:T(8,128)S(1)}, bf16[3072,1536]{1,0:T(8,128)(2,1)S(1)}, bf16[3072,1536]{1,0:T(8,128)(2,1)S(1)}) custom-call(f32[2,12,16,128]{3,2,1,0:T(8,128)S(1)} %collective-permute-done.8.refs_0_, f32[2,12,16,128]{3,2,1,0:T(8,128)S(1)} %collective-permute-done.9.refs_1_, ...), custom_call_target="tpu_custom_call", output_to_operand_aliasing={{1}: (4, {}), {2}: (5, {})} | custom-call | flops 1811939328 | bytes 4194304 | tf_op jit(solution)/shard_map/pallas_call | solution.py:130
  36.8 2.9 %collective-permute-start.14 = (f32[12,16,128]{2,1,0:T(8,128)S(1)}, f32[12,16,128]{2,1,0:T(8,128)S(1)}, u32[]{:S(2)}, u32[]{:S(2)}) collective-permute-start(f32[12,16,128]{2,1,0:T(8,128)S(1)} %get-tuple-element.64), channel_id=1, source_target_pairs={{0,24},{1,25},{2,26},{3,27},{4,28},{5,29},{6,30},{7,31},{8,16},{9,... | collective-permute-start | bytes 294920 | tf_op jit(solution)/shard_map/ppermute | solution.py:184
  40.1 0.4 collective-permute-start.13
  40.7 2.8 %collective-permute-done.14 = f32[12,16,128]{2,1,0:T(8,128)S(1)} collective-permute-done((f32[12,16,128]{2,1,0:T(8,128)S(1)}, f32[12,16,128]{2,1,0:T(8,128)S(1)}, u32[]{:S(2)}, u32[]{:S(2)}) %collective-permute-start.14) | collective-permute-done | bytes 98336 | tf_op jit(solution)/shard_map/ppermute | solution.py:184
  43.4 1.3 collective-permute-done.12
  44.9 7.8 %collective-permute-start.16 = (f32[2,12,16,128]{3,2,1,0:T(8,128)S(1)}, f32[2,12,16,128]{3,2,1,0:T(8,128)S(1)}, u32[]{:S(2)}, u32[]{:S(2)}) collective-permute-start(f32[2,12,16,128]{3,2,1,0:T(8,128)S(1)} %pad_maximum_fusion.2), channel_id=1, source_target_pairs={{0,6},{1,1},{2,14},{3,9},{4,22},{5,17},{6,30},{7,25},{8,4},{9,3},{... | collective-permute-start | bytes 589832 | tf_op jit(solution)/shard_map/ppermute | solution.py:184
  52.8 1.1 collective-permute-start.17
  53.9 4.0 %collective-permute-start.24 = (f32[2,12,16,128]{3,2,1,0:T(8,128)S(1)}, f32[2,12,16,128]{3,2,1,0:T(8,128)S(1)}, u32[]{:S(2)}, u32[]{:S(2)}) collective-permute-start(f32[2,12,16,128]{3,2,1,0:T(8,128)S(1)} %pad_maximum_fusion.3), channel_id=1, source_target_pairs={{0,6},{1,1},{2,14},{3,9},{4,22},{5,17},{6,30},{7,25},{8,4},{9,3},{... | collective-permute-start | bytes 589832 | tf_op jit(solution)/shard_map/ppermute | solution.py:184
  58.3 1.9 %collective-permute-done.17.refs_1_ = f32[2,12,16,128]{3,2,1,0:T(8,128)S(1)} collective-permute-done((f32[2,12,16,128]{3,2,1,0:T(8,128)S(1)}, f32[2,12,16,128]{3,2,1,0:T(8,128)S(1)}, u32[]{:S(2)}, u32[]{:S(2)}) %collective-permute-start.17) | collective-permute-done | bytes 196640 | tf_op jit(solution)/shard_map/ppermute | solution.py:184
  60.7 2.1 %collective-permute-done.24.refs_0_ = f32[2,12,16,128]{3,2,1,0:T(8,128)S(1)} collective-permute-done((f32[2,12,16,128]{3,2,1,0:T(8,128)S(1)}, f32[2,12,16,128]{3,2,1,0:T(8,128)S(1)}, u32[]{:S(2)}, u32[]{:S(2)}) %collective-permute-start.24) | collective-permute-done | bytes 196640 | tf_op jit(solution)/shard_map/ppermute | solution.py:184
  62.9 2.0 %collective-permute-done.25.refs_1_ = f32[2,12,16,128]{3,2,1,0:T(8,128)S(1)} collective-permute-done((f32[2,12,16,128]{3,2,1,0:T(8,128)S(1)}, f32[2,12,16,128]{3,2,1,0:T(8,128)S(1)}, u32[]{:S(2)}, u32[]{:S(2)}) %collective-permute-start.25) | collective-permute-done | bytes 196640 | tf_op jit(solution)/shard_map/ppermute | solution.py:184
  64.9 3.0 %shard_map.44 = (f32[4,12,16,128]{3,2,1,0:T(8,128)S(1)}, bf16[3072,1536]{1,0:T(8,128)(2,1)S(1)}, bf16[3072,1536]{1,0:T(8,128)(2,1)S(1)}) custom-call(f32[2,12,16,128]{3,2,1,0:T(8,128)S(1)} %collective-permute-done.16.refs_0_, f32[2,12,16,128]{3,2,1,0:T(8,128)S(1)} %collective-permute-done.17.refs_1_, ...), custom_call_target="tpu_custom_call", output_to_operand_aliasing={{1}: (4, {}), {2}: (5, {})} | custom-call | flops 1811939328 | bytes 4194304 | tf_op jit(solution)/shard_map/pallas_call | solution.py:130
  67.9 4.9 %collective-permute-start.22 = (f32[12,16,128]{2,1,0:T(8,128)S(1)}, f32[12,16,128]{2,1,0:T(8,128)S(1)}, u32[]{:S(2)}, u32[]{:S(2)}) collective-permute-start(f32[12,16,128]{2,1,0:T(8,128)S(1)} %get-tuple-element.60), channel_id=1, source_target_pairs={{0,24},{1,25},{2,26},{3,27},{4,28},{5,29},{6,30},{7,31},{8,16},{9,... | collective-permute-start | bytes 294920 | tf_op jit(solution)/shard_map/ppermute | solution.py:184
  72.9 5.3 %collective-permute-start.20 = (f32[12,16,128]{2,1,0:T(8,128)S(1)}, f32[12,16,128]{2,1,0:T(8,128)S(1)}, u32[]{:S(2)}, u32[]{:S(2)}) collective-permute-start(f32[12,16,128]{2,1,0:T(8,128)S(1)} %get-tuple-element.61), channel_id=1, source_target_pairs={{0,8},{1,9},{2,10},{3,11},{4,12},{5,13},{6,14},{7,15},{8,0},{9,1},... | collective-permute-start | bytes 294920 | tf_op jit(solution)/shard_map/ppermute | solution.py:184
  78.2 3.0 %shard_map.47 = (f32[4,12,16,128]{3,2,1,0:T(8,128)S(1)}, bf16[3072,1536]{1,0:T(8,128)(2,1)S(1)}, bf16[3072,1536]{1,0:T(8,128)(2,1)S(1)}) custom-call(f32[2,12,16,128]{3,2,1,0:T(8,128)S(1)} %collective-permute-done.24.refs_0_, f32[2,12,16,128]{3,2,1,0:T(8,128)S(1)} %collective-permute-done.25.refs_1_, ...), custom_call_target="tpu_custom_call", output_to_operand_aliasing={{1}: (4, {}), {2}: (5, {})} | custom-call | flops 1811939328 | bytes 4194304 | tf_op jit(solution)/shard_map/pallas_call | solution.py:130
  81.3 1.5 %collective-permute-start.30 = (f32[12,16,128]{2,1,0:T(8,128)S(1)}, f32[12,16,128]{2,1,0:T(8,128)S(1)}, u32[]{:S(2)}, u32[]{:S(2)}) collective-permute-start(f32[12,16,128]{2,1,0:T(8,128)S(1)} %get-tuple-element.56), channel_id=1, source_target_pairs={{0,24},{1,25},{2,26},{3,27},{4,28},{5,29},{6,30},{7,31},{8,16},{9,... | collective-permute-start | bytes 294920 | tf_op jit(solution)/shard_map/ppermute | solution.py:184
  82.8 2.0 %collective-permute-start.28 = (f32[12,16,128]{2,1,0:T(8,128)S(1)}, f32[12,16,128]{2,1,0:T(8,128)S(1)}, u32[]{:S(2)}, u32[]{:S(2)}) collective-permute-start(f32[12,16,128]{2,1,0:T(8,128)S(1)} %get-tuple-element.57), channel_id=1, source_target_pairs={{0,8},{1,9},{2,10},{3,11},{4,12},{5,13},{6,14},{7,15},{8,0},{9,1},... | collective-permute-start | bytes 294920 | tf_op jit(solution)/shard_map/ppermute | solution.py:184
  85.1 2.5 %collective-permute-done.30 = f32[12,16,128]{2,1,0:T(8,128)S(1)} collective-permute-done((f32[12,16,128]{2,1,0:T(8,128)S(1)}, f32[12,16,128]{2,1,0:T(8,128)S(1)}, u32[]{:S(2)}, u32[]{:S(2)}) %collective-permute-start.30) | collective-permute-done | bytes 98336 | tf_op jit(solution)/shard_map/ppermute | solution.py:184
  87.6 1.2 collective-permute-done.28
  88.8 0.8 collective-permute-done.29
  89.7 4.7 %collective-permute-start.32 = (f32[2,12,16,128]{3,2,1,0:T(8,128)S(1)}, f32[2,12,16,128]{3,2,1,0:T(8,128)S(1)}, u32[]{:S(2)}, u32[]{:S(2)}) collective-permute-start(f32[2,12,16,128]{3,2,1,0:T(8,128)S(1)} %pad_maximum_fusion.4), channel_id=1, source_target_pairs={{0,6},{1,1},{2,14},{3,9},{4,22},{5,17},{6,30},{7,25},{8,4},{9,3},{... | collective-permute-start | bytes 589832 | tf_op jit(solution)/shard_map/ppermute | solution.py:184
  94.4 1.1 collective-permute-start.33
  95.5 3.5 %collective-permute-start.40 = (f32[2,12,16,128]{3,2,1,0:T(8,128)S(1)}, f32[2,12,16,128]{3,2,1,0:T(8,128)S(1)}, u32[]{:S(2)}, u32[]{:S(2)}) collective-permute-start(f32[2,12,16,128]{3,2,1,0:T(8,128)S(1)} %pad_maximum_fusion.5), channel_id=1, source_target_pairs={{0,6},{1,1},{2,14},{3,9},{4,22},{5,17},{6,30},{7,25},{8,4},{9,3},{... | collective-permute-start | bytes 589832 | tf_op jit(solution)/shard_map/ppermute | solution.py:184
  99.0 1.4 %collective-permute-start.41 = (f32[2,12,16,128]{3,2,1,0:T(8,128)S(1)}, f32[2,12,16,128]{3,2,1,0:T(8,128)S(1)}, u32[]{:S(2)}, u32[]{:S(2)}) collective-permute-start(f32[2,12,16,128]{3,2,1,0:T(8,128)S(1)} %pad_maximum_fusion.5), channel_id=1, source_target_pairs={{0,4},{1,3},{2,12},{3,11},{4,20},{5,19},{6,28},{7,27},{8,6},{9,1},... | collective-permute-start | bytes 589832 | tf_op jit(solution)/shard_map/ppermute | solution.py:184
  100.4 1.5 %collective-permute-done.33.refs_1_ = f32[2,12,16,128]{3,2,1,0:T(8,128)S(1)} collective-permute-done((f32[2,12,16,128]{3,2,1,0:T(8,128)S(1)}, f32[2,12,16,128]{3,2,1,0:T(8,128)S(1)}, u32[]{:S(2)}, u32[]{:S(2)}) %collective-permute-start.33) | collective-permute-done | bytes 196640 | tf_op jit(solution)/shard_map/ppermute | solution.py:184
  102.5 1.7 %collective-permute-done.40.refs_0_ = f32[2,12,16,128]{3,2,1,0:T(8,128)S(1)} collective-permute-done((f32[2,12,16,128]{3,2,1,0:T(8,128)S(1)}, f32[2,12,16,128]{3,2,1,0:T(8,128)S(1)}, u32[]{:S(2)}, u32[]{:S(2)}) %collective-permute-start.40) | collective-permute-done | bytes 196640 | tf_op jit(solution)/shard_map/ppermute | solution.py:184
  104.2 2.0 %collective-permute-done.41.refs_1_ = f32[2,12,16,128]{3,2,1,0:T(8,128)S(1)} collective-permute-done((f32[2,12,16,128]{3,2,1,0:T(8,128)S(1)}, f32[2,12,16,128]{3,2,1,0:T(8,128)S(1)}, u32[]{:S(2)}, u32[]{:S(2)}) %collective-permute-start.41) | collective-permute-done | bytes 196640 | tf_op jit(solution)/shard_map/ppermute | solution.py:184
  106.2 3.0 %shard_map.50 = (f32[4,12,16,128]{3,2,1,0:T(8,128)S(1)}, bf16[3072,1536]{1,0:T(8,128)(2,1)S(1)}, bf16[3072,1536]{1,0:T(8,128)(2,1)S(1)}) custom-call(f32[2,12,16,128]{3,2,1,0:T(8,128)S(1)} %collective-permute-done.32.refs_0_, f32[2,12,16,128]{3,2,1,0:T(8,128)S(1)} %collective-permute-done.33.refs_1_, ...), custom_call_target="tpu_custom_call", output_to_operand_aliasing={{1}: (4, {}), {2}: (5, {})} | custom-call | flops 1811939328 | bytes 4194304 | tf_op jit(solution)/shard_map/pallas_call | solution.py:130
  109.2 5.0 %collective-permute-start.38 = (f32[12,16,128]{2,1,0:T(8,128)S(1)}, f32[12,16,128]{2,1,0:T(8,128)S(1)}, u32[]{:S(2)}, u32[]{:S(2)}) collective-permute-start(f32[12,16,128]{2,1,0:T(8,128)S(1)} %get-tuple-element.52), channel_id=1, source_target_pairs={{0,24},{1,25},{2,26},{3,27},{4,28},{5,29},{6,30},{7,31},{8,16},{9,... | collective-permute-start | bytes 294920 | tf_op jit(solution)/shard_map/ppermute | solution.py:184
  114.2 4.6 %collective-permute-start.36 = (f32[12,16,128]{2,1,0:T(8,128)S(1)}, f32[12,16,128]{2,1,0:T(8,128)S(1)}, u32[]{:S(2)}, u32[]{:S(2)}) collective-permute-start(f32[12,16,128]{2,1,0:T(8,128)S(1)} %get-tuple-element.53), channel_id=1, source_target_pairs={{0,8},{1,9},{2,10},{3,11},{4,12},{5,13},{6,14},{7,15},{8,0},{9,1},... | collective-permute-start | bytes 294920 | tf_op jit(solution)/shard_map/ppermute | solution.py:184
  118.8 3.0 %shard_map.53 = (f32[4,12,16,128]{3,2,1,0:T(8,128)S(1)}, bf16[3072,1536]{1,0:T(8,128)(2,1)S(1)}, bf16[3072,1536]{1,0:T(8,128)(2,1)S(1)}) custom-call(f32[2,12,16,128]{3,2,1,0:T(8,128)S(1)} %collective-permute-done.40.refs_0_, f32[2,12,16,128]{3,2,1,0:T(8,128)S(1)} %collective-permute-done.41.refs_1_, ...), custom_call_target="tpu_custom_call", output_to_operand_aliasing={{1}: (4, {}), {2}: (5, {})} | custom-call | flops 1811939328 | bytes 4194304 | tf_op jit(solution)/shard_map/pallas_call | solution.py:130
  121.9 1.5 %collective-permute-start.46 = (f32[12,16,128]{2,1,0:T(8,128)S(1)}, f32[12,16,128]{2,1,0:T(8,128)S(1)}, u32[]{:S(2)}, u32[]{:S(2)}) collective-permute-start(f32[12,16,128]{2,1,0:T(8,128)S(1)} %get-tuple-element.48), channel_id=1, source_target_pairs={{0,24},{1,25},{2,26},{3,27},{4,28},{5,29},{6,30},{7,31},{8,16},{9,... | collective-permute-start | bytes 294920 | tf_op jit(solution)/shard_map/ppermute | solution.py:184
  123.4 2.0 %collective-permute-start.44 = (f32[12,16,128]{2,1,0:T(8,128)S(1)}, f32[12,16,128]{2,1,0:T(8,128)S(1)}, u32[]{:S(2)}, u32[]{:S(2)}) collective-permute-start(f32[12,16,128]{2,1,0:T(8,128)S(1)} %get-tuple-element.49), channel_id=1, source_target_pairs={{0,8},{1,9},{2,10},{3,11},{4,12},{5,13},{6,14},{7,15},{8,0},{9,1},... | collective-permute-start | bytes 294920 | tf_op jit(solution)/shard_map/ppermute | solution.py:184
  125.6 2.5 %collective-permute-done.46 = f32[12,16,128]{2,1,0:T(8,128)S(1)} collective-permute-done((f32[12,16,128]{2,1,0:T(8,128)S(1)}, f32[12,16,128]{2,1,0:T(8,128)S(1)}, u32[]{:S(2)}, u32[]{:S(2)}) %collective-permute-start.46) | collective-permute-done | bytes 98336 | tf_op jit(solution)/shard_map/ppermute | solution.py:184
  128.1 1.2 collective-permute-done.44
  129.4 0.8 collective-permute-done.45
  130.2 0.8 copy-done.1
  (90 shorter events, 4.1 us)
Async XLA Ops:
  0.0 1.8 %collective-permute-start = (f32[12,32,128]{2,1,0:T(8,128)}, f32[12,32,128]{2,1,0:T(8,128)S(1)}, u32[]{:S(2)}, u32[]{:S(2)}) collective-permute-start(f32[12,32,128]{2,1,0:T(8,128)} %bitcast.78), channel_id=1, source_target_pairs={{0,1},{1,0},{2,3},{3,2},{4,5},{5,4},{6,7},{7,6},{8,9},{9,8},{10,11... | collective-permute-start | bytes 589832 | tf_op jit(solution)/shard_map/ppermute | solution.py:184
  1.8 11.9 %collective-permute-start.1 = (f32[2,12,16,128]{3,2,1,0:T(8,128)S(1)}, f32[2,12,16,128]{3,2,1,0:T(8,128)S(1)}, u32[]{:S(2)}, u32[]{:S(2)}) collective-permute-start(f32[2,12,16,128]{3,2,1,0:T(8,128)S(1)} %pad_maximum_fusion), channel_id=1, source_target_pairs={{0,6},{1,1},{2,14},{3,9},{4,22},{5,17},{6,30},{7,25},{8,4},{9,3},{... | collective-permute-start | bytes 589832 | tf_op jit(solution)/shard_map/ppermute | solution.py:184
  8.7 7.8 %collective-permute-start.2 = (f32[2,12,16,128]{3,2,1,0:T(8,128)S(1)}, f32[2,12,16,128]{3,2,1,0:T(8,128)S(1)}, u32[]{:S(2)}, u32[]{:S(2)}) collective-permute-start(f32[2,12,16,128]{3,2,1,0:T(8,128)S(1)} %pad_maximum_fusion), channel_id=1, source_target_pairs={{0,4},{1,3},{2,12},{3,11},{4,20},{5,19},{6,28},{7,27},{8,6},{9,1},... | collective-permute-start | bytes 589832 | tf_op jit(solution)/shard_map/ppermute | solution.py:184
  10.3 13.3 %copy-start = (f32[128,128]{1,0:T(8,128)S(1)}, f32[128,128]{1,0:T(8,128)}, u32[]{:S(2)}) copy-start(f32[128,128]{1,0:T(8,128)} %hamiltonian.11) | copy-start | bytes 196612
  10.3 13.8 %collective-permute-start.8 = (f32[2,12,16,128]{3,2,1,0:T(8,128)S(1)}, f32[2,12,16,128]{3,2,1,0:T(8,128)S(1)}, u32[]{:S(2)}, u32[]{:S(2)}) collective-permute-start(f32[2,12,16,128]{3,2,1,0:T(8,128)S(1)} %pad_maximum_fusion.1), channel_id=1, source_target_pairs={{0,6},{1,1},{2,14},{3,9},{4,22},{5,17},{6,30},{7,25},{8,4},{9,3},{... | collective-permute-start | bytes 589832 | tf_op jit(solution)/shard_map/ppermute | solution.py:184
  13.5 11.3 %collective-permute-start.9 = (f32[2,12,16,128]{3,2,1,0:T(8,128)S(1)}, f32[2,12,16,128]{3,2,1,0:T(8,128)S(1)}, u32[]{:S(2)}, u32[]{:S(2)}) collective-permute-start(f32[2,12,16,128]{3,2,1,0:T(8,128)S(1)} %pad_maximum_fusion.1), channel_id=1, source_target_pairs={{0,4},{1,3},{2,12},{3,11},{4,20},{5,19},{6,28},{7,27},{8,6},{9,1},... | collective-permute-start | bytes 589832 | tf_op jit(solution)/shard_map/ppermute | solution.py:184
  13.7 11.1 %collective-permute-start.3 = (f32[2,12,16,128]{3,2,1,0:T(8,128)S(1)}, f32[2,12,16,128]{3,2,1,0:T(8,128)S(1)}, u32[]{:S(2)}, u32[]{:S(2)}) collective-permute-start(f32[2,12,16,128]{3,2,1,0:T(8,128)S(1)} %collective-permute-done.1.refs_0_), channel_id=1, source_target_pairs={{0,1},{1,0},{2,3},{3,2},{4,5},{5,4},{6,7},{7,6},{8,9},{9,8},{10,11... | collective-permute-start | bytes 589832 | tf_op jit(solution)/shard_map/ppermute | solution.py:184
  16.5 8.3 %collective-permute-start.4 = (f32[2,12,16,128]{3,2,1,0:T(8,128)S(1)}, f32[2,12,16,128]{3,2,1,0:T(8,128)S(1)}, u32[]{:S(2)}, u32[]{:S(2)}) collective-permute-start(f32[2,12,16,128]{3,2,1,0:T(8,128)S(1)} %collective-permute-done.2.refs_1_), channel_id=1, source_target_pairs={{0,1},{1,0},{2,3},{3,2},{4,5},{5,4},{6,7},{7,6},{8,9},{9,8},{10,11... | collective-permute-start | bytes 589832 | tf_op jit(solution)/shard_map/ppermute | solution.py:184
  24.1 9.6 %collective-permute-start.10 = (f32[2,12,16,128]{3,2,1,0:T(8,128)S(1)}, f32[2,12,16,128]{3,2,1,0:T(8,128)S(1)}, u32[]{:S(2)}, u32[]{:S(2)}) collective-permute-start(f32[2,12,16,128]{3,2,1,0:T(8,128)S(1)} %collective-permute-done.8.refs_0_), channel_id=1, source_target_pairs={{0,1},{1,0},{2,3},{3,2},{4,5},{5,4},{6,7},{7,6},{8,9},{9,8},{10,11... | collective-permute-start | bytes 589832 | tf_op jit(solution)/shard_map/ppermute | solution.py:184
  24.7 9.1 %collective-permute-start.11 = (f32[2,12,16,128]{3,2,1,0:T(8,128)S(1)}, f32[2,12,16,128]{3,2,1,0:T(8,128)S(1)}, u32[]{:S(2)}, u32[]{:S(2)}) collective-permute-start(f32[2,12,16,128]{3,2,1,0:T(8,128)S(1)} %collective-permute-done.9.refs_1_), channel_id=1, source_target_pairs={{0,1},{1,0},{2,3},{3,2},{4,5},{5,4},{6,7},{7,6},{8,9},{9,8},{10,11... | collective-permute-start | bytes 589832 | tf_op jit(solution)/shard_map/ppermute | solution.py:184
  27.8 12.2 %collective-permute-start.7 = (f32[12,16,128]{2,1,0:T(8,128)S(1)}, f32[12,16,128]{2,1,0:T(8,128)S(1)}, u32[]{:S(2)}, u32[]{:S(2)}) collective-permute-start(f32[12,16,128]{2,1,0:T(8,128)S(1)} %get-tuple-element.68), channel_id=1, source_target_pairs={{0,24},{1,25},{2,26},{3,27},{4,28},{5,29},{6,30},{7,31},{8,16},{9,... | collective-permute-start | bytes 294920 | tf_op jit(solution)/shard_map/ppermute | solution.py:184
  33.1 7.4 %collective-permute-start.5 = (f32[12,16,128]{2,1,0:T(8,128)S(1)}, f32[12,16,128]{2,1,0:T(8,128)S(1)}, u32[]{:S(2)}, u32[]{:S(2)}) collective-permute-start(f32[12,16,128]{2,1,0:T(8,128)S(1)} %get-tuple-element.69), channel_id=1, source_target_pairs={{0,8},{1,9},{2,10},{3,11},{4,12},{5,13},{6,14},{7,15},{8,0},{9,1},... | collective-permute-start | bytes 294920 | tf_op jit(solution)/shard_map/ppermute | solution.py:184
  33.4 7.1 %collective-permute-start.6 = (f32[12,16,128]{2,1,0:T(8,128)S(1)}, f32[12,16,128]{2,1,0:T(8,128)S(1)}, u32[]{:S(2)}, u32[]{:S(2)}) collective-permute-start(f32[12,16,128]{2,1,0:T(8,128)S(1)} %get-tuple-element.67), channel_id=1, source_target_pairs={{0,16},{1,17},{2,18},{3,19},{4,20},{5,21},{6,22},{7,23},{8,24},{9,... | collective-permute-start | bytes 294920 | tf_op jit(solution)/shard_map/ppermute | solution.py:184
  36.8 6.6 %collective-permute-start.14 = (f32[12,16,128]{2,1,0:T(8,128)S(1)}, f32[12,16,128]{2,1,0:T(8,128)S(1)}, u32[]{:S(2)}, u32[]{:S(2)}) collective-permute-start(f32[12,16,128]{2,1,0:T(8,128)S(1)} %get-tuple-element.64), channel_id=1, source_target_pairs={{0,24},{1,25},{2,26},{3,27},{4,28},{5,29},{6,30},{7,31},{8,16},{9,... | collective-permute-start | bytes 294920 | tf_op jit(solution)/shard_map/ppermute | solution.py:184
  39.7 5.0 %collective-permute-start.12 = (f32[12,16,128]{2,1,0:T(8,128)S(1)}, f32[12,16,128]{2,1,0:T(8,128)S(1)}, u32[]{:S(2)}, u32[]{:S(2)}) collective-permute-start(f32[12,16,128]{2,1,0:T(8,128)S(1)} %get-tuple-element.65), channel_id=1, source_target_pairs={{0,8},{1,9},{2,10},{3,11},{4,12},{5,13},{6,14},{7,15},{8,0},{9,1},... | collective-permute-start | bytes 294920 | tf_op jit(solution)/shard_map/ppermute | solution.py:184
  40.1 4.7 %collective-permute-start.13 = (f32[12,16,128]{2,1,0:T(8,128)S(1)}, f32[12,16,128]{2,1,0:T(8,128)S(1)}, u32[]{:S(2)}, u32[]{:S(2)}) collective-permute-start(f32[12,16,128]{2,1,0:T(8,128)S(1)} %get-tuple-element.63), channel_id=1, source_target_pairs={{0,16},{1,17},{2,18},{3,19},{4,20},{5,21},{6,22},{7,23},{8,24},{9,... | collective-permute-start | bytes 294920 | tf_op jit(solution)/shard_map/ppermute | solution.py:184
  40.5 4.4 %collective-permute-start.15 = (f32[12,16,128]{2,1,0:T(8,128)S(1)}, f32[12,16,128]{2,1,0:T(8,128)S(1)}, u32[]{:S(2)}, u32[]{:S(2)}) collective-permute-start(f32[12,16,128]{2,1,0:T(8,128)S(1)} %multiply_subtract_fusion.3.value), channel_id=1, source_target_pairs={{0,1},{1,0},{2,3},{3,2},{4,5},{5,4},{6,7},{7,6},{8,9},{9,8},{10,11... | collective-permute-start | bytes 294920 | tf_op jit(solution)/shard_map/ppermute | solution.py:184
  44.8 9.1 %collective-permute-start.23 = (f32[12,16,128]{2,1,0:T(8,128)S(1)}, f32[12,16,128]{2,1,0:T(8,128)S(1)}, u32[]{:S(2)}, u32[]{:S(2)}) collective-permute-start(f32[12,16,128]{2,1,0:T(8,128)S(1)} %get-tuple-element.46.value), channel_id=1, source_target_pairs={{0,1},{1,0},{2,3},{3,2},{4,5},{5,4},{6,7},{7,6},{8,9},{9,8},{10,11... | collective-permute-start | bytes 294920 | tf_op jit(solution)/shard_map/ppermute | solution.py:184
  44.9 13.3 %collective-permute-start.16 = (f32[2,12,16,128]{3,2,1,0:T(8,128)S(1)}, f32[2,12,16,128]{3,2,1,0:T(8,128)S(1)}, u32[]{:S(2)}, u32[]{:S(2)}) collective-permute-start(f32[2,12,16,128]{3,2,1,0:T(8,128)S(1)} %pad_maximum_fusion.2), channel_id=1, source_target_pairs={{0,6},{1,1},{2,14},{3,9},{4,22},{5,17},{6,30},{7,25},{8,4},{9,3},{... | collective-permute-start | bytes 589832 | tf_op jit(solution)/shard_map/ppermute | solution.py:184
  52.8 7.5 %collective-permute-start.17 = (f32[2,12,16,128]{3,2,1,0:T(8,128)S(1)}, f32[2,12,16,128]{3,2,1,0:T(8,128)S(1)}, u32[]{:S(2)}, u32[]{:S(2)}) collective-permute-start(f32[2,12,16,128]{3,2,1,0:T(8,128)S(1)} %pad_maximum_fusion.2), channel_id=1, source_target_pairs={{0,4},{1,3},{2,12},{3,11},{4,20},{5,19},{6,28},{7,27},{8,6},{9,1},... | collective-permute-start | bytes 589832 | tf_op jit(solution)/shard_map/ppermute | solution.py:184
  53.9 9.0 %collective-permute-start.24 = (f32[2,12,16,128]{3,2,1,0:T(8,128)S(1)}, f32[2,12,16,128]{3,2,1,0:T(8,128)S(1)}, u32[]{:S(2)}, u32[]{:S(2)}) collective-permute-start(f32[2,12,16,128]{3,2,1,0:T(8,128)S(1)} %pad_maximum_fusion.3), channel_id=1, source_target_pairs={{0,6},{1,1},{2,14},{3,9},{4,22},{5,17},{6,30},{7,25},{8,4},{9,3},{... | collective-permute-start | bytes 589832 | tf_op jit(solution)/shard_map/ppermute | solution.py:184
  58.0 6.9 %collective-permute-start.25 = (f32[2,12,16,128]{3,2,1,0:T(8,128)S(1)}, f32[2,12,16,128]{3,2,1,0:T(8,128)S(1)}, u32[]{:S(2)}, u32[]{:S(2)}) collective-permute-start(f32[2,12,16,128]{3,2,1,0:T(8,128)S(1)} %pad_maximum_fusion.3), channel_id=1, source_target_pairs={{0,4},{1,3},{2,12},{3,11},{4,20},{5,19},{6,28},{7,27},{8,6},{9,1},... | collective-permute-start | bytes 589832 | tf_op jit(solution)/shard_map/ppermute | solution.py:184
  58.2 6.7 %collective-permute-start.18 = (f32[2,12,16,128]{3,2,1,0:T(8,128)S(1)}, f32[2,12,16,128]{3,2,1,0:T(8,128)S(1)}, u32[]{:S(2)}, u32[]{:S(2)}) collective-permute-start(f32[2,12,16,128]{3,2,1,0:T(8,128)S(1)} %collective-permute-done.16.refs_0_), channel_id=1, source_target_pairs={{0,1},{1,0},{2,3},{3,2},{4,5},{5,4},{6,7},{7,6},{8,9},{9,8},{10,11... | collective-permute-start | bytes 589832 | tf_op jit(solution)/shard_map/ppermute | solution.py:184
  60.2 4.7 %collective-permute-start.19 = (f32[2,12,16,128]{3,2,1,0:T(8,128)S(1)}, f32[2,12,16,128]{3,2,1,0:T(8,128)S(1)}, u32[]{:S(2)}, u32[]{:S(2)}) collective-permute-start(f32[2,12,16,128]{3,2,1,0:T(8,128)S(1)} %collective-permute-done.17.refs_1_), channel_id=1, source_target_pairs={{0,1},{1,0},{2,3},{3,2},{4,5},{5,4},{6,7},{7,6},{8,9},{9,8},{10,11... | collective-permute-start | bytes 589832 | tf_op jit(solution)/shard_map/ppermute | solution.py:184
  62.9 15.3 %collective-permute-start.26 = (f32[2,12,16,128]{3,2,1,0:T(8,128)S(1)}, f32[2,12,16,128]{3,2,1,0:T(8,128)S(1)}, u32[]{:S(2)}, u32[]{:S(2)}) collective-permute-start(f32[2,12,16,128]{3,2,1,0:T(8,128)S(1)} %collective-permute-done.24.refs_0_), channel_id=1, source_target_pairs={{0,1},{1,0},{2,3},{3,2},{4,5},{5,4},{6,7},{7,6},{8,9},{9,8},{10,11... | collective-permute-start | bytes 589832 | tf_op jit(solution)/shard_map/ppermute | solution.py:184
  64.9 13.3 %collective-permute-start.27 = (f32[2,12,16,128]{3,2,1,0:T(8,128)S(1)}, f32[2,12,16,128]{3,2,1,0:T(8,128)S(1)}, u32[]{:S(2)}, u32[]{:S(2)}) collective-permute-start(f32[2,12,16,128]{3,2,1,0:T(8,128)S(1)} %collective-permute-done.25.refs_1_), channel_id=1, source_target_pairs={{0,1},{1,0},{2,3},{3,2},{4,5},{5,4},{6,7},{7,6},{8,9},{9,8},{10,11... | collective-permute-start | bytes 589832 | tf_op jit(solution)/shard_map/ppermute | solution.py:184
  67.9 16.9 %collective-permute-start.22 = (f32[12,16,128]{2,1,0:T(8,128)S(1)}, f32[12,16,128]{2,1,0:T(8,128)S(1)}, u32[]{:S(2)}, u32[]{:S(2)}) collective-permute-start(f32[12,16,128]{2,1,0:T(8,128)S(1)} %get-tuple-element.60), channel_id=1, source_target_pairs={{0,24},{1,25},{2,26},{3,27},{4,28},{5,29},{6,30},{7,31},{8,16},{9,... | collective-permute-start | bytes 294920 | tf_op jit(solution)/shard_map/ppermute | solution.py:184
  72.9 12.1 %collective-permute-start.20 = (f32[12,16,128]{2,1,0:T(8,128)S(1)}, f32[12,16,128]{2,1,0:T(8,128)S(1)}, u32[]{:S(2)}, u32[]{:S(2)}) collective-permute-start(f32[12,16,128]{2,1,0:T(8,128)S(1)} %get-tuple-element.61), channel_id=1, source_target_pairs={{0,8},{1,9},{2,10},{3,11},{4,12},{5,13},{6,14},{7,15},{8,0},{9,1},... | collective-permute-start | bytes 294920 | tf_op jit(solution)/shard_map/ppermute | solution.py:184
  78.2 6.8 %collective-permute-start.21 = (f32[12,16,128]{2,1,0:T(8,128)S(1)}, f32[12,16,128]{2,1,0:T(8,128)S(1)}, u32[]{:S(2)}, u32[]{:S(2)}) collective-permute-start(f32[12,16,128]{2,1,0:T(8,128)S(1)} %get-tuple-element.59), channel_id=1, source_target_pairs={{0,16},{1,17},{2,18},{3,19},{4,20},{5,21},{6,22},{7,23},{8,24},{9,... | collective-permute-start | bytes 294920 | tf_op jit(solution)/shard_map/ppermute | solution.py:184
  81.3 6.3 %collective-permute-start.30 = (f32[12,16,128]{2,1,0:T(8,128)S(1)}, f32[12,16,128]{2,1,0:T(8,128)S(1)}, u32[]{:S(2)}, u32[]{:S(2)}) collective-permute-start(f32[12,16,128]{2,1,0:T(8,128)S(1)} %get-tuple-element.56), channel_id=1, source_target_pairs={{0,24},{1,25},{2,26},{3,27},{4,28},{5,29},{6,30},{7,31},{8,16},{9,... | collective-permute-start | bytes 294920 | tf_op jit(solution)/shard_map/ppermute | solution.py:184
  82.8 6.0 %collective-permute-start.28 = (f32[12,16,128]{2,1,0:T(8,128)S(1)}, f32[12,16,128]{2,1,0:T(8,128)S(1)}, u32[]{:S(2)}, u32[]{:S(2)}) collective-permute-start(f32[12,16,128]{2,1,0:T(8,128)S(1)} %get-tuple-element.57), channel_id=1, source_target_pairs={{0,8},{1,9},{2,10},{3,11},{4,12},{5,13},{6,14},{7,15},{8,0},{9,1},... | collective-permute-start | bytes 294920 | tf_op jit(solution)/shard_map/ppermute | solution.py:184
  84.9 4.7 %collective-permute-start.29 = (f32[12,16,128]{2,1,0:T(8,128)S(1)}, f32[12,16,128]{2,1,0:T(8,128)S(1)}, u32[]{:S(2)}, u32[]{:S(2)}) collective-permute-start(f32[12,16,128]{2,1,0:T(8,128)S(1)} %get-tuple-element.55), channel_id=1, source_target_pairs={{0,16},{1,17},{2,18},{3,19},{4,20},{5,21},{6,22},{7,23},{8,24},{9,... | collective-permute-start | bytes 294920 | tf_op jit(solution)/shard_map/ppermute | solution.py:184
  85.0 4.7 %collective-permute-start.31 = (f32[12,16,128]{2,1,0:T(8,128)S(1)}, f32[12,16,128]{2,1,0:T(8,128)S(1)}, u32[]{:S(2)}, u32[]{:S(2)}) collective-permute-start(f32[12,16,128]{2,1,0:T(8,128)S(1)} %get-tuple-element.44.value), channel_id=1, source_target_pairs={{0,1},{1,0},{2,3},{3,2},{4,5},{5,4},{6,7},{7,6},{8,9},{9,8},{10,11... | collective-permute-start | bytes 294920 | tf_op jit(solution)/shard_map/ppermute | solution.py:184
  89.6 5.9 %collective-permute-start.39 = (f32[12,16,128]{2,1,0:T(8,128)S(1)}, f32[12,16,128]{2,1,0:T(8,128)S(1)}, u32[]{:S(2)}, u32[]{:S(2)}) collective-permute-start(f32[12,16,128]{2,1,0:T(8,128)S(1)} %get-tuple-element.42.value), channel_id=1, source_target_pairs={{0,1},{1,0},{2,3},{3,2},{4,5},{5,4},{6,7},{7,6},{8,9},{9,8},{10,11... | collective-permute-start | bytes 294920 | tf_op jit(solution)/shard_map/ppermute | solution.py:184
  89.7 10.7 %collective-permute-start.32 = (f32[2,12,16,128]{3,2,1,0:T(8,128)S(1)}, f32[2,12,16,128]{3,2,1,0:T(8,128)S(1)}, u32[]{:S(2)}, u32[]{:S(2)}) collective-permute-start(f32[2,12,16,128]{3,2,1,0:T(8,128)S(1)} %pad_maximum_fusion.4), channel_id=1, source_target_pairs={{0,6},{1,1},{2,14},{3,9},{4,22},{5,17},{6,30},{7,25},{8,4},{9,3},{... | collective-permute-start | bytes 589832 | tf_op jit(solution)/shard_map/ppermute | solution.py:184
  94.4 7.5 %collective-permute-start.33 = (f32[2,12,16,128]{3,2,1,0:T(8,128)S(1)}, f32[2,12,16,128]{3,2,1,0:T(8,128)S(1)}, u32[]{:S(2)}, u32[]{:S(2)}) collective-permute-start(f32[2,12,16,128]{3,2,1,0:T(8,128)S(1)} %pad_maximum_fusion.4), channel_id=1, source_target_pairs={{0,4},{1,3},{2,12},{3,11},{4,20},{5,19},{6,28},{7,27},{8,6},{9,1},... | collective-permute-start | bytes 589832 | tf_op jit(solution)/shard_map/ppermute | solution.py:184
  95.5 8.7 %collective-permute-start.40 = (f32[2,12,16,128]{3,2,1,0:T(8,128)S(1)}, f32[2,12,16,128]{3,2,1,0:T(8,128)S(1)}, u32[]{:S(2)}, u32[]{:S(2)}) collective-permute-start(f32[2,12,16,128]{3,2,1,0:T(8,128)S(1)} %pad_maximum_fusion.5), channel_id=1, source_target_pairs={{0,6},{1,1},{2,14},{3,9},{4,22},{5,17},{6,30},{7,25},{8,4},{9,3},{... | collective-permute-start | bytes 589832 | tf_op jit(solution)/shard_map/ppermute | solution.py:184
  99.0 7.2 %collective-permute-start.41 = (f32[2,12,16,128]{3,2,1,0:T(8,128)S(1)}, f32[2,12,16,128]{3,2,1,0:T(8,128)S(1)}, u32[]{:S(2)}, u32[]{:S(2)}) collective-permute-start(f32[2,12,16,128]{3,2,1,0:T(8,128)S(1)} %pad_maximum_fusion.5), channel_id=1, source_target_pairs={{0,4},{1,3},{2,12},{3,11},{4,20},{5,19},{6,28},{7,27},{8,6},{9,1},... | collective-permute-start | bytes 589832 | tf_op jit(solution)/shard_map/ppermute | solution.py:184
  100.4 5.8 %collective-permute-start.34 = (f32[2,12,16,128]{3,2,1,0:T(8,128)S(1)}, f32[2,12,16,128]{3,2,1,0:T(8,128)S(1)}, u32[]{:S(2)}, u32[]{:S(2)}) collective-permute-start(f32[2,12,16,128]{3,2,1,0:T(8,128)S(1)} %collective-permute-done.32.refs_0_), channel_id=1, source_target_pairs={{0,1},{1,0},{2,3},{3,2},{4,5},{5,4},{6,7},{7,6},{8,9},{9,8},{10,11... | collective-permute-start | bytes 589832 | tf_op jit(solution)/shard_map/ppermute | solution.py:184
  102.0 4.2 %collective-permute-start.35 = (f32[2,12,16,128]{3,2,1,0:T(8,128)S(1)}, f32[2,12,16,128]{3,2,1,0:T(8,128)S(1)}, u32[]{:S(2)}, u32[]{:S(2)}) collective-permute-start(f32[2,12,16,128]{3,2,1,0:T(8,128)S(1)} %collective-permute-done.33.refs_1_), channel_id=1, source_target_pairs={{0,1},{1,0},{2,3},{3,2},{4,5},{5,4},{6,7},{7,6},{8,9},{9,8},{10,11... | collective-permute-start | bytes 589832 | tf_op jit(solution)/shard_map/ppermute | solution.py:184
  104.2 14.6 %collective-permute-start.42 = (f32[2,12,16,128]{3,2,1,0:T(8,128)S(1)}, f32[2,12,16,128]{3,2,1,0:T(8,128)S(1)}, u32[]{:S(2)}, u32[]{:S(2)}) collective-permute-start(f32[2,12,16,128]{3,2,1,0:T(8,128)S(1)} %collective-permute-done.40.refs_0_), channel_id=1, source_target_pairs={{0,1},{1,0},{2,3},{3,2},{4,5},{5,4},{6,7},{7,6},{8,9},{9,8},{10,11... | collective-permute-start | bytes 589832 | tf_op jit(solution)/shard_map/ppermute | solution.py:184
  106.2 12.6 %collective-permute-start.43 = (f32[2,12,16,128]{3,2,1,0:T(8,128)S(1)}, f32[2,12,16,128]{3,2,1,0:T(8,128)S(1)}, u32[]{:S(2)}, u32[]{:S(2)}) collective-permute-start(f32[2,12,16,128]{3,2,1,0:T(8,128)S(1)} %collective-permute-done.41.refs_1_), channel_id=1, source_target_pairs={{0,1},{1,0},{2,3},{3,2},{4,5},{5,4},{6,7},{7,6},{8,9},{9,8},{10,11... | collective-permute-start | bytes 589832 | tf_op jit(solution)/shard_map/ppermute | solution.py:184
  109.2 16.2 %collective-permute-start.38 = (f32[12,16,128]{2,1,0:T(8,128)S(1)}, f32[12,16,128]{2,1,0:T(8,128)S(1)}, u32[]{:S(2)}, u32[]{:S(2)}) collective-permute-start(f32[12,16,128]{2,1,0:T(8,128)S(1)} %get-tuple-element.52), channel_id=1, source_target_pairs={{0,24},{1,25},{2,26},{3,27},{4,28},{5,29},{6,30},{7,31},{8,16},{9,... | collective-permute-start | bytes 294920 | tf_op jit(solution)/shard_map/ppermute | solution.py:184
  114.2 11.3 %collective-permute-start.36 = (f32[12,16,128]{2,1,0:T(8,128)S(1)}, f32[12,16,128]{2,1,0:T(8,128)S(1)}, u32[]{:S(2)}, u32[]{:S(2)}) collective-permute-start(f32[12,16,128]{2,1,0:T(8,128)S(1)} %get-tuple-element.53), channel_id=1, source_target_pairs={{0,8},{1,9},{2,10},{3,11},{4,12},{5,13},{6,14},{7,15},{8,0},{9,1},... | collective-permute-start | bytes 294920 | tf_op jit(solution)/shard_map/ppermute | solution.py:184
  118.8 6.8 %collective-permute-start.37 = (f32[12,16,128]{2,1,0:T(8,128)S(1)}, f32[12,16,128]{2,1,0:T(8,128)S(1)}, u32[]{:S(2)}, u32[]{:S(2)}) collective-permute-start(f32[12,16,128]{2,1,0:T(8,128)S(1)} %get-tuple-element.51), channel_id=1, source_target_pairs={{0,16},{1,17},{2,18},{3,19},{4,20},{5,21},{6,22},{7,23},{8,24},{9,... | collective-permute-start | bytes 294920 | tf_op jit(solution)/shard_map/ppermute | solution.py:184
  121.9 6.3 %collective-permute-start.46 = (f32[12,16,128]{2,1,0:T(8,128)S(1)}, f32[12,16,128]{2,1,0:T(8,128)S(1)}, u32[]{:S(2)}, u32[]{:S(2)}) collective-permute-start(f32[12,16,128]{2,1,0:T(8,128)S(1)} %get-tuple-element.48), channel_id=1, source_target_pairs={{0,24},{1,25},{2,26},{3,27},{4,28},{5,29},{6,30},{7,31},{8,16},{9,... | collective-permute-start | bytes 294920 | tf_op jit(solution)/shard_map/ppermute | solution.py:184
  123.4 6.0 %collective-permute-start.44 = (f32[12,16,128]{2,1,0:T(8,128)S(1)}, f32[12,16,128]{2,1,0:T(8,128)S(1)}, u32[]{:S(2)}, u32[]{:S(2)}) collective-permute-start(f32[12,16,128]{2,1,0:T(8,128)S(1)} %get-tuple-element.49), channel_id=1, source_target_pairs={{0,8},{1,9},{2,10},{3,11},{4,12},{5,13},{6,14},{7,15},{8,0},{9,1},... | collective-permute-start | bytes 294920 | tf_op jit(solution)/shard_map/ppermute | solution.py:184
  125.5 4.7 %collective-permute-start.45 = (f32[12,16,128]{2,1,0:T(8,128)S(1)}, f32[12,16,128]{2,1,0:T(8,128)S(1)}, u32[]{:S(2)}, u32[]{:S(2)}) collective-permute-start(f32[12,16,128]{2,1,0:T(8,128)S(1)} %get-tuple-element.47), channel_id=1, source_target_pairs={{0,16},{1,17},{2,18},{3,19},{4,20},{5,21},{6,22},{7,23},{8,24},{9,... | collective-permute-start | bytes 294920 | tf_op jit(solution)/shard_map/ppermute | solution.py:184
  (1 other events, 0.8 us)
